TPU v7x, 512 devices: a whole 4x8x8 slice. The times are simulated.
512 devices in a mesh: genome: 128 (over z, y, core), tower: 4 (over x).
Axes of the slice: x: 4, y: 8, z: 8, core: 2. Of those that a mesh axis runs over, the one named last changes fastest.
Arguments:
- genome_bases: int32 [16777216], P('genome'), may hold values from 0 to 3
- stitch_weight: int32 [256], replicated, may hold values from 1 to 8
- stem_weight: bfloat16 [96, 8192], replicated, may hold values from -0.125 to 0.125
- trunk_in: bfloat16 [6, 48, 288], replicated, may hold values from -0.375 to 0.375
- trunk_out: bfloat16 [6, 96, 48], replicated, may hold values from -0.875 to 0.875
- pair_weight: bfloat16 [96, 96], replicated, may hold values from -0.625 to 0.625
- distance_rate: float32 [48], replicated, may hold values from 0.05 to 0.3
- tower_conv: bfloat16 [2, 3, 48, 144], replicated, may hold values from -0.3125 to 0.3125
- tower_mix: bfloat16 [2, 48, 48], replicated, may hold values from -0.875 to 0.875
- head_weight: bfloat16 [5, 48], replicated, may hold values from -0.875 to 0.875
Outputs:
- stitched: float32 [5, 8192, 256], P(None, ('genome', 'tower'))
- scores: float32 [2, 5, 8192], P(None, None, ('genome', 'tower'))
All inputs are finite; a program needn't handle non-finite values.
Results may differ from a plain program's by a relative error of at most 0.019.
Values may be sent and summed in bfloat16 or wider, within the bound.
A program may use at most 64 MiB of HBM per device.

v0:
```python
import jax
import jax.numpy as jnp
from jax import lax
from jax.sharding import PartitionSpec as P

BP = 2048
STRIDE = 64
BINS = 256


def from_behind(block, axis, distance):
    devices = range(lax.axis_size(axis))
    route = [(i - distance, i) for i in devices if i - distance in devices]
    return lax.ppermute(block, axis, route)


def padded_2(block, sides, width):
    for axis, dim in sides:
        count = lax.axis_size(axis)
        forward = [(i, i + 1) for i in range(count - 1)]
        forward.append((count - 1, 0))
        backward = [(target, source) for source, target in forward]
        low = lax.ppermute(
            lax.slice_in_dim(block, block.shape[dim] - width, None, axis=dim), axis, forward
        )
        high = lax.ppermute(lax.slice_in_dim(block, 0, width, axis=dim), axis, backward)
        block = jnp.concatenate([low, block, high], axis=dim)
    return block


def as_sent(value):
    return jax.tree.map(lambda a: a.astype(jnp.bfloat16) if a.dtype == jnp.float32 else a, value)


def shift_cols(values, offset):
    extent = values.shape[-1]
    margins = [(0, 0)] * (values.ndim - 1)
    if offset >= 0:
        padded = jnp.pad(values, margins + [(0, offset)])
        return padded[..., offset : offset + extent]
    padded = jnp.pad(values, margins + [(-offset, 0)])
    return padded[..., :extent]


def stem_features(genome_bases, stem_weight):
    letters = genome_bases.reshape(-1, BP)
    onehot = (letters[:, :, None] == jnp.arange(4, dtype=jnp.int32)[None, None, :]).astype(
        jnp.bfloat16
    )
    onehot = onehot.reshape(letters.shape[0], 4 * BP)
    summed = lax.dot_general(
        stem_weight, onehot, (((1,), (1,)), ((), ())), preferred_element_type=jnp.float32
    )
    return summed.astype(jnp.bfloat16)


def trunk_stream(window, trunk_in, trunk_out):
    stream = window.astype(jnp.float32)
    layers = trunk_in.shape[0]
    extent = window.shape[-1]
    for layer_index in range(layers):
        dilation = max(1, extent // 2 ** (layers - layer_index))
        active = jax.nn.relu(stream).astype(jnp.bfloat16)
        stacked = jnp.concatenate(
            [shift_cols(active, -dilation), active, shift_cols(active, dilation)], axis=0
        )
        inner = jnp.dot(trunk_in[layer_index], stacked, preferred_element_type=jnp.float32)
        squeezed = jax.nn.relu(inner).astype(jnp.bfloat16)
        stream = stream + jnp.dot(
            trunk_out[layer_index], squeezed, preferred_element_type=jnp.float32
        )
    return stream


def conv_rows(active, kernel):
    height = active.shape[2] - 2
    extent = active.shape[3]
    padded = jnp.pad(active, ((0, 0), (0, 0), (0, 0), (1, 1)))
    summed = None
    for row_tap in range(3):
        stacked = jnp.concatenate(
            [
                padded[:, :, row_tap : row_tap + height, col_tap : col_tap + extent]
                for col_tap in range(3)
            ],
            axis=0,
        )
        partial_value = jnp.einsum(
            "oc,ckrj->okrj", kernel[row_tap], stacked, preferred_element_type=jnp.float32
        )
        summed = partial_value if summed is None else summed + partial_value
    return summed


def build_pair(projected, distance_rate, tower_index, height, margin):
    channels = distance_rate.shape[0]
    left_padded = jnp.pad(projected[:channels], ((0, 0), (margin, margin)))
    right_cols = projected[channels:]
    col_pos = jnp.arange(BINS)
    pair_blocks = []
    for block_index in range(BINS // STRIDE):
        start_row = STRIDE * block_index + height * tower_index - margin
        left_rows = lax.dynamic_slice_in_dim(
            left_padded, start_row + margin, height + 2 * margin, axis=1
        )
        row_pos = start_row + jnp.arange(height + 2 * margin)
        separation = jnp.abs(row_pos[:, None] - col_pos[None, :]).astype(jnp.float32)
        inside = ((row_pos >= 0) & (row_pos < BINS)).astype(jnp.float32)
        mixed = (
            left_rows[:, :, None]
            + right_cols[:, None, :]
            - distance_rate[:, None, None] * jnp.log1p(separation)[None]
        )
        pair_blocks.append((jax.nn.relu(mixed) * inside[None, :, None]).astype(jnp.bfloat16))
    return jnp.stack(pair_blocks, axis=1)


def skew_rows(rows_map, first_row):
    targets = rows_map.shape[0]
    height = rows_map.shape[1]
    extent = rows_map.shape[2]
    padded = jnp.pad(rows_map, ((0, 0), (0, 0), (0, extent)))
    flattened = padded.reshape(targets, height * 2 * extent)
    flattened = jnp.pad(flattened, ((0, 0), (0, extent + height)))
    sliced = lax.dynamic_slice_in_dim(flattened, first_row, height * (2 * extent + 1), axis=1)
    return sliced.reshape(targets, height, 2 * extent + 1)[:, :, :extent]


def per_device(
    genome_bases,
    stitch_weight,
    stem_weight,
    trunk_in,
    trunk_out,
    pair_weight,
    distance_rate,
    tower_conv,
    tower_mix,
    head_weight,
):
    blocks = BINS // STRIDE
    towers = lax.axis_size("tower")
    height = STRIDE // towers
    tower_index = lax.axis_index("tower")
    genome_index = lax.axis_index("genome")
    own_features = stem_features(genome_bases, stem_weight)
    gathered = [own_features]
    for distance in range(1, blocks):
        gathered.append(from_behind(own_features, "genome", -distance))
    window = jnp.concatenate(gathered, axis=1)
    stream = trunk_stream(window, trunk_in, trunk_out)
    projected = jnp.dot(
        pair_weight, jax.nn.relu(stream).astype(jnp.bfloat16), preferred_element_type=jnp.float32
    )
    layers = tower_conv.shape[0]
    pair_map = build_pair(projected, distance_rate, tower_index, height, 1)
    tower_stream = pair_map[:, :, 1:-1].astype(jnp.float32)
    active = pair_map
    for layer_index in range(layers):
        if layer_index > 0:
            inner_act = jax.nn.relu(tower_stream).astype(jnp.bfloat16)
            widened = padded_2(inner_act, (("tower", 2),), 1)
            lower_rim = widened[:, :, :1]
            upper_rim = widened[:, :, -1:]
            zero_block = jnp.zeros_like(lower_rim[:, :1])
            lower_rim = jnp.where(
                tower_index == 0,
                jnp.concatenate([zero_block, lower_rim[:, :-1]], axis=1),
                lower_rim,
            )
            upper_rim = jnp.where(
                tower_index == towers - 1,
                jnp.concatenate([upper_rim[:, 1:], zero_block], axis=1),
                upper_rim,
            )
            active = jnp.concatenate([lower_rim, inner_act, upper_rim], axis=2)
        convolved = conv_rows(active, tower_conv[layer_index])
        squeezed = jax.nn.relu(convolved).astype(jnp.bfloat16)
        tower_stream = tower_stream + jnp.einsum(
            "oc,ckrj->okrj", tower_mix[layer_index], squeezed, preferred_element_type=jnp.float32
        )
    final_act = jax.nn.relu(tower_stream).astype(jnp.bfloat16)
    contact_maps = jnp.einsum(
        "tc,ckrj->tkrj", head_weight, final_act, preferred_element_type=jnp.float32
    )
    weights_float = stitch_weight.astype(jnp.float32)
    offsets = jnp.arange(BINS)
    local_rows = jnp.arange(height)
    pieces = []
    weight_sum = jnp.zeros((height, BINS), jnp.float32)
    for block_index in range(blocks):
        first_row = STRIDE * block_index + height * tower_index
        skewed = skew_rows(contact_maps[:, block_index], first_row)
        row_weight = lax.dynamic_slice_in_dim(weights_float, first_row, height)
        pieces.append(skewed * row_weight[None, :, None])
        covered = (genome_index >= block_index) & (
            first_row + local_rows[:, None] + offsets[None, :] < BINS
        )
        weight_sum = weight_sum + jnp.where(covered, row_weight[:, None], 0.0)
    weighted = pieces[0]
    for block_index in range(1, blocks):
        weighted = weighted + from_behind(
            pieces[block_index].astype(jnp.bfloat16), "genome", block_index
        ).astype(jnp.float32)
    stitched = weighted / jnp.maximum(weight_sum, 1.0)[None]
    head_cols = stitched[:, :, : 2 * STRIDE]
    received = []
    for distance in range(towers, 0, -1):
        received.append(
            from_behind(as_sent(head_cols), ("genome", "tower"), distance).astype(head_cols.dtype)
        )
    previous = jnp.concatenate(received, axis=1)
    extended = jnp.concatenate([previous, head_cols], axis=1)
    targets = extended.shape[0]
    prefix = jnp.concatenate(
        [jnp.zeros((targets, STRIDE + height, 1), jnp.float32), jnp.cumsum(extended, axis=2)],
        axis=2,
    )
    square = prefix[:, :, STRIDE + 1 : 2 * STRIDE + 1] - prefix[:, :, 1 : STRIDE + 1]
    contact = jnp.exp(extended[:, :, 1 : STRIDE + 1])
    row_pos = jnp.arange(STRIDE + height)
    col_pos = jnp.arange(STRIDE)
    out_row = jnp.arange(height)
    pick_square = (
        row_pos[None, :, None] == STRIDE + out_row[:, None, None] - col_pos[None, None, :]
    ).astype(jnp.float32)
    pick_up = (
        row_pos[None, :, None] == STRIDE + out_row[:, None, None] - col_pos[None, None, :] - 1
    ).astype(jnp.float32)
    insulation = jnp.einsum("txa,rxa->tr", square, pick_square, precision=lax.Precision.HIGHEST) / (
        STRIDE * STRIDE
    )
    upstream = jnp.einsum("txa,rxa->tr", contact, pick_up, precision=lax.Precision.HIGHEST)
    downstream = jnp.sum(contact[:, STRIDE:], axis=2)
    direction = (downstream - upstream) / (downstream + upstream)
    return (stitched, jnp.stack([insulation, direction]))


def solution(mesh):
    placed = (P("genome"), P(), P(), P(), P(), P(), P(), P(), P(), P())
    return jax.shard_map(
        per_device,
        mesh=mesh,
        in_specs=placed,
        out_specs=(P(None, ("genome", "tower"), None), P(None, None, ("genome", "tower"))),
        check_vma=False,
    )
```

profile of v0, /device:TPU:256, one launch (start us, length us, event | category | flops | bytes accessed | tf_op | source)
XLA Modules:
  0.0 109.9 jit_solution(12108818006245739050)
XLA Ops:
  0.6 1.2 %eq.54 = s32[64,2048]{1,0:T(8,128)S(1)} reshape(s32[131072]{0:T(1024)} %param.10) | data formatting | bytes 1048576 | tf_op jit(solution)/shard_map/eq | solution.py:47
  1.9 0.3 copy.61
  2.2 1.1 eq.57
  3.3 1.8 %eq.58 = s32[8192]{0:T(1024)S(1)} reshape(s32[2048,4]{1,0:T(8,128)} %eq.57) | data formatting | bytes 65536 | tf_op jit(solution)/shard_map/eq | solution.py:47
  5.1 0.8 eq.55
  5.9 2.1 %fusion.79 = bf16[96,64]{0,1:T(8,128)(2,1)S(1)} fusion(bf16[96,8192]{1,0:T(8,128)(2,1)S(1)} %copy-done, s32[64,8192]{0,1:T(8,128)S(1)} %bitcast.217, s32[8192]{0:T(1024)S(1)} %eq.58), kind=kOutput, calls=%fused_computation.97 | convolution fusion | flops 101718016 | bytes 3715072 | tf_op jit(solution)/shard_map/dot_general | solution.py:51
  8.1 3.9 %collective-permute-start = (bf16[96,64]{0,1:T(8,128)(2,1)S(1)}, bf16[96,64]{0,1:T(8,128)(2,1)S(1)}, u32[]{:S(2)}, u32[]{:S(2)}) collective-permute-start(bf16[96,64]{0,1:T(8,128)(2,1)S(1)} %fusion.79), channel_id=1, source_target_pairs={{4,0},{8,4},{12,8},{16,12},{20,16},{24,20},{28,24},{32,28},{36,32}... | collective-permute-start | bytes 36872 | tf_op jit(solution)/shard_map/ppermute | solution.py:14
  12.0 3.3 %collective-permute-start.1 = (bf16[96,64]{0,1:T(8,128)(2,1)S(1)}, bf16[96,64]{0,1:T(8,128)(2,1)S(1)}, u32[]{:S(2)}, u32[]{:S(2)}) collective-permute-start(bf16[96,64]{0,1:T(8,128)(2,1)S(1)} %fusion.79), channel_id=1, source_target_pairs={{8,0},{12,4},{16,8},{20,12},{24,16},{28,20},{32,24},{36,28},{40,32... | collective-permute-start | bytes 36872 | tf_op jit(solution)/shard_map/ppermute | solution.py:14
  15.2 3.1 %collective-permute-start.2 = (bf16[96,64]{0,1:T(8,128)(2,1)S(1)}, bf16[96,64]{0,1:T(8,128)(2,1)S(1)}, u32[]{:S(2)}, u32[]{:S(2)}) collective-permute-start(bf16[96,64]{0,1:T(8,128)(2,1)S(1)} %fusion.79), channel_id=1, source_target_pairs={{12,0},{16,4},{20,8},{24,12},{28,16},{32,20},{36,24},{40,28},{44,3... | collective-permute-start | bytes 36872 | tf_op jit(solution)/shard_map/ppermute | solution.py:14
  18.5 0.1 convert_log-plus-one_fusion
  18.6 0.1 convert_log-plus-one_fusion.2
  18.9 1.4 %collective-permute-done.2 = bf16[96,64]{0,1:T(8,128)(2,1)S(1)} collective-permute-done((bf16[96,64]{0,1:T(8,128)(2,1)S(1)}, bf16[96,64]{0,1:T(8,128)(2,1)S(1)}, u32[]{:S(2)}, u32[]{:S(2)}) %collective-permute-start.2) | collective-permute-done | bytes 12320 | tf_op jit(solution)/shard_map/ppermute | solution.py:14
  20.4 0.5 maximum_convert_fusion.7
  20.9 0.5 maximum_convert_fusion.6
  21.4 0.5 maximum_convert_fusion.5
  21.9 0.5 maximum_convert_fusion.4
  22.4 0.5 maximum_convert_fusion.3
  22.9 0.3 fusion.77
  23.2 0.3 convolution_bitcast_fusion.7
  23.6 0.1 pad_dynamic-slice_fusion.7
  24.0 1.0 multiply_convert_fusion.3
  25.1 0.2 pad_maximum_fusion.2
  25.3 5.1 %pad_slice_fusion.1 = (bf16[48,4,16,256]{3,0,2,1:T(8,128)(2,1)}, bf16[48,4,16,256]{3,0,2,1:T(8,128)(2,1)S(1)}, bf16[48,4,16,256]{3,0,2,1:T(8,128)(2,1)S(1)}, bf1...) fusion(bf16[48,4,18,256]{3,0,2,1:T(8,128)(2,1)S(1)} %pad_maximu, ...), kind=kLoop, calls=%fused_computation.43 | loop fusion | bytes 20643840 | tf_op jit(solution)/shard_map/slice | solution.py:83
  30.4 2.2 %fusion.17 = f32[4,16,256,48]{2,3,1,0:T(8,128)} fusion(bf16[48,4,16,256]{3,0,2,1:T(8,128)(2,1)S(1)} %get-tuple-element.19, bf16[48,4,16,256]{3,0,2,1:T(8,128)(2,1)S(1)} %get-tuple-element.24, bf16[48,4,16,256]{3,0,2,1:T(8,128)(2,1)S(1)} %get-tuple-element.18, bf16[2,3,48,144]{3,2,1,0:T(8,128)(2,1)S(1)} %copy-done.9), kind=kOutput, calls=%fused_computation.19 | convolution fusion | flops 240648192 | bytes 7888896 | tf_op jit(solution)/shard_map/oc,ckrj->okrj/dot_general | solution.py:88
  32.6 2.2 %fusion.11 = f32[4,16,256,48]{2,3,1,0:T(8,128)} fusion(bf16[48,4,16,256]{3,0,2,1:T(8,128)(2,1)S(1)} %get-tuple-element.17, bf16[48,4,16,256]{3,0,2,1:T(8,128)(2,1)S(1)} %get-tuple-element.22, bf16[48,4,16,256]{3,0,2,1:T(8,128)(2,1)S(1)} %get-tuple-element.23, bf16[2,3,48,144]{3,2,1,0:T(8,128)(2,1)S(1)} %copy-done.9), kind=kOutput, calls=%fused_computation.13 | convolution fusion | flops 240648192 | bytes 7888896 | tf_op jit(solution)/shard_map/oc,ckrj->okrj/dot_general | solution.py:88
  34.8 6.2 %maximum_convert_fusion.1 = (bf16[48,4,16,256]{3,0,2,1:T(8,128)(2,1)S(1)}, f32[4,16,256,48]{2,3,1,0:T(8,128)}) fusion(bf16[48,4,18,256]{3,0,2,1:T(8,128)(2,1)S(1)} %pad_maximum_fusion.2, bf16[48,4,16,256]{3,0,2,1:T(8,128)(2,1)} %get-tuple-element.20, bf16[48,4,16,256]{3,0,2,1:T(8,128)(2,1)} %get-tuple-element.21, ...), kind=kOutput, calls=%fused_computation.53 | convolution fusion | flops 322437120 | bytes 17338368 | tf_op jit(solution)/shard_map/oc,ckrj->okrj/dot_general | solution.py:179
  41.0 3.4 %collective-permute-start.3 = (bf16[48,4,1,256]{3,0,2,1:T(8,128)(2,1)S(1)}, bf16[48,4,1,256]{3,0,2,1:T(8,128)(2,1)S(1)}, u32[]{:S(2)}, u32[]{:S(2)}) collective-permute-start(bf16[48,4,1,256]{3,0,2,1:T(8,128)(2,1)S(1)} %get-tuple-element.25), channel_id=1, source_target_pairs={{0,1},{1,2},{2,3},{3,0},{4,5},{5,6},{6,7},{7,4},{8,9},{9,10},{10,1... | collective-permute-start | bytes 294920 | tf_op jit(solution)/shard_map/ppermute | solution.py:23
  44.4 3.8 %collective-permute-start.4 = (bf16[48,4,1,256]{3,0,2,1:T(8,128)(2,1)S(1)}, bf16[48,4,1,256]{3,0,2,1:T(8,128)(2,1)S(1)}, u32[]{:S(2)}, u32[]{:S(2)}) collective-permute-start(bf16[48,4,1,256]{3,0,2,1:T(8,128)(2,1)S(1)} %get-tuple-element.26), channel_id=1, source_target_pairs={{1,0},{2,1},{3,2},{0,3},{5,4},{6,5},{7,6},{4,7},{9,8},{10,9},{11,1... | collective-permute-start | bytes 294920 | tf_op jit(solution)/shard_map/ppermute | solution.py:26
  48.2 0.9 collective-permute-done.3
  49.2 1.9 %collective-permute-done.4 = bf16[48,4,1,256]{3,0,2,1:T(8,128)(2,1)S(1)} collective-permute-done((bf16[48,4,1,256]{3,0,2,1:T(8,128)(2,1)S(1)}, bf16[48,4,1,256]{3,0,2,1:T(8,128)(2,1)S(1)}, u32[]{:S(2)}, u32[]{:S(2)}) %collective-permute-start.4) | collective-permute-done | bytes 98336 | tf_op jit(solution)/shard_map/ppermute | solution.py:26
  51.1 1.8 %fusion.45 = bf16[48,4,18,258]{3,0,2,1:T(8,128)(2,1)S(1)} fusion(bf16[48,4,1,256]{3,0,2,1:T(8,128)(2,1)S(1)} %pad_select_fusion, bf16[48,4,16,256]{3,0,2,1:T(8,128)(2,1)S(1)} %get-tuple-element.69, bf16[48,4,1,256]{3,0,2,1:T(8,128)(2,1)S(1)} %pad_select_fusion.1), kind=kLoop, calls=%fused_computation.59 | loop fusion | flops 10699776 | bytes 3552768 | tf_op jit(solution)/shard_map/concatenate | solution.py:176
  53.0 4.0 %fusion.242 = (bf16[48,4,16,256]{3,0,2,1:T(8,128)(2,1)}, bf16[48,4,16,256]{3,0,2,1:T(8,128)(2,1)S(1)}, bf16[48,4,16,256]{3,0,2,1:T(8,128)(2,1)}, bf16[48,4,16,25...) fusion(bf16[48,4,18,258]{3,0,2,1:T(8,128)(2,1)S(1)} %fusion.45), kind=kLoop, calls=%fused_computation.291 | loop fusion | bytes 18874368 | tf_op jit(solution)/shard_map/slice | solution.py:83
  57.0 2.2 %fusion.8 = f32[4,16,256,48]{2,3,1,0:T(8,128)} fusion(bf16[48,4,16,256]{3,0,2,1:T(8,128)(2,1)S(1)} %get-tuple-element.69, bf16[48,4,1,256]{3,0,2,1:T(8,128)(2,1)S(1)} %pad_select_fusion.1, bf16[48,4,16,256]{3,0,2,1:T(8,128)(2,1)S(1)} %get-tuple-element.13, bf16[48,4,16,256]{3,0,2,1:T(8,128)(2,1)S(1)} %get-tuple-element.14, ...), kind=kOutput, calls=%fused_computation.11 | convolution fusion | flops 245366784 | bytes 7987200 | tf_op jit(solution)/shard_map/oc,ckrj->okrj/dot_general | solution.py:88
  59.1 2.2 %fusion.3 = f32[4,16,256,48]{2,3,1,0:T(8,128)} fusion(bf16[48,4,1,256]{3,0,2,1:T(8,128)(2,1)S(1)} %pad_select_fusion, bf16[48,4,16,256]{3,0,2,1:T(8,128)(2,1)S(1)} %get-tuple-element.69, bf16[48,4,16,256]{3,0,2,1:T(8,128)(2,1)S(1)} %get-tuple-element.15, bf16[48,4,16,256]{3,0,2,1:T(8,128)(2,1)S(1)} %get-tuple-element.11, ...), kind=kOutput, calls=%fused_computation.6 | convolution fusion | flops 245366784 | bytes 7987200 | tf_op jit(solution)/shard_map/oc,ckrj->okrj/dot_general | solution.py:88
  61.3 6.4 %fusion.40 = bf16[48,4,16,256]{3,0,2,1:T(8,128)(2,1)} fusion(f32[4,16,256,48]{2,3,1,0:T(8,128)} %get-tuple-element.70, f32[4,16,256,48]{2,3,1,0:T(8,128)} %fusion.3, f32[4,16,256,48]{2,3,1,0:T(8,128)} %fusion.8, bf16[48,4,16,256]{3,0,2,1:T(8,128)(2,1)} %get-tuple-element.12, bf16[48,4,16,256]{3,0,2,1:T(8,128)(2,1)S(1)} %get-tuple-element.69, ...), kind=kOutput, calls=%fused_computation.50 | convolution fusion | flops 323223552 | bytes 17338368 | tf_op jit(solution)/shard_map/oc,ckrj->okrj/dot_general | solution.py:179
  67.7 1.7 %convolution_bitcast_fusion = f32[5,4,16,256]{3,0,2,1:T(8,128)S(1)} fusion(bf16[48,4,16,256]{3,0,2,1:T(8,128)(2,1)} %fusion.40, bf16[5,48]{1,0:T(8,128)(2,1)S(1)} %copy-done.4), kind=kOutput, calls=%fused_computation.68 | convolution fusion | flops 7864320 | bytes 1901024 | tf_op jit(solution)/shard_map/tc,ckrj->tkrj/dot_general | solution.py:183
  69.5 0.1 pad_dynamic-slice_fusion.2
  69.7 0.2 reshape.466
  69.9 1.9 %collective-permute-start.5 = (bf16[5,16,256]{2,1,0:T(8,128)(2,1)S(1)}, bf16[5,16,256]{2,1,0:T(8,128)(2,1)S(1)}, u32[]{:S(2)}, u32[]{:S(2)}) collective-permute-start(bf16[5,16,256]{2,1,0:T(8,128)(2,1)S(1)} %fusion.142), channel_id=1, source_target_pairs={{0,4},{4,8},{8,12},{12,16},{16,20},{20,24},{24,28},{28,32},{32,36}... | collective-permute-start | bytes 122888 | tf_op jit(solution)/shard_map/ppermute | solution.py:14
  71.8 0.1 pad_dynamic-slice_fusion.1
  72.0 0.2 reshape.468
  72.2 2.4 %collective-permute-start.6 = (bf16[5,16,256]{2,1,0:T(8,128)(2,1)S(1)}, bf16[5,16,256]{2,1,0:T(8,128)(2,1)S(1)}, u32[]{:S(2)}, u32[]{:S(2)}) collective-permute-start(bf16[5,16,256]{2,1,0:T(8,128)(2,1)S(1)} %fusion.141), channel_id=1, source_target_pairs={{0,8},{4,12},{8,16},{12,20},{16,24},{20,28},{24,32},{28,36},{32,40... | collective-permute-start | bytes 122888 | tf_op jit(solution)/shard_map/ppermute | solution.py:14
  74.6 0.1 pad_dynamic-slice_fusion
  74.8 0.2 reshape.470
  75.0 4.6 %collective-permute-start.7 = (bf16[5,16,256]{2,1,0:T(8,128)(2,1)S(1)}, bf16[5,16,256]{2,1,0:T(8,128)(2,1)S(1)}, u32[]{:S(2)}, u32[]{:S(2)}) collective-permute-start(bf16[5,16,256]{2,1,0:T(8,128)(2,1)S(1)} %fusion.140), channel_id=1, source_target_pairs={{0,12},{4,16},{8,20},{12,24},{16,28},{20,32},{24,36},{28,40},{32,4... | collective-permute-start | bytes 122888 | tf_op jit(solution)/shard_map/ppermute | solution.py:14
  79.7 0.1 pad_dynamic-slice_fusion.3
  79.8 0.2 reshape.464
  80.0 1.5 %collective-permute-done.6 = bf16[5,16,256]{2,1,0:T(8,128)(2,1)S(1)} collective-permute-done((bf16[5,16,256]{2,1,0:T(8,128)(2,1)S(1)}, bf16[5,16,256]{2,1,0:T(8,128)(2,1)S(1)}, u32[]{:S(2)}, u32[]{:S(2)}) %collective-permute-start.6) | collective-permute-done | bytes 40992 | tf_op jit(solution)/shard_map/ppermute | solution.py:14
  81.5 3.2 %collective-permute-done.7 = bf16[5,16,256]{2,1,0:T(8,128)(2,1)S(1)} collective-permute-done((bf16[5,16,256]{2,1,0:T(8,128)(2,1)S(1)}, bf16[5,16,256]{2,1,0:T(8,128)(2,1)S(1)}, u32[]{:S(2)}, u32[]{:S(2)}) %collective-permute-start.7) | collective-permute-done | bytes 40992 | tf_op jit(solution)/shard_map/ppermute | solution.py:14
  84.8 2.0 %collective-permute-start.8 = (bf16[5,16,128]{2,1,0:T(8,128)(2,1)S(1)}, bf16[5,16,128]{2,1,0:T(8,128)(2,1)S(1)}, u32[]{:S(2)}, u32[]{:S(2)}) collective-permute-start(bf16[5,16,128]{2,1,0:T(8,128)(2,1)S(1)} %slice.459), channel_id=1, source_target_pairs={{0,4},{1,5},{2,6},{3,7},{4,8},{5,9},{6,10},{7,11},{8,12},{9,13},{1... | collective-permute-start | bytes 61448 | tf_op jit(solution)/shard_map/ppermute | solution.py:14
  86.8 4.9 %collective-permute-start.9 = (bf16[5,16,128]{2,1,0:T(8,128)(2,1)S(1)}, bf16[5,16,128]{2,1,0:T(8,128)(2,1)S(1)}, u32[]{:S(2)}, u32[]{:S(2)}) collective-permute-start(bf16[5,16,128]{2,1,0:T(8,128)(2,1)S(1)} %slice.459), channel_id=1, source_target_pairs={{0,3},{1,4},{2,5},{3,6},{4,7},{5,8},{6,9},{7,10},{8,11},{9,12},{10... | collective-permute-start | bytes 61448 | tf_op jit(solution)/shard_map/ppermute | solution.py:14
  91.7 3.6 %collective-permute-start.10 = (bf16[5,16,128]{2,1,0:T(8,128)(2,1)S(1)}, bf16[5,16,128]{2,1,0:T(8,128)(2,1)S(1)}, u32[]{:S(2)}, u32[]{:S(2)}) collective-permute-start(bf16[5,16,128]{2,1,0:T(8,128)(2,1)S(1)} %slice.459), channel_id=1, source_target_pairs={{0,2},{1,3},{2,4},{3,5},{4,6},{5,7},{6,8},{7,9},{8,10},{9,11},{10,... | collective-permute-start | bytes 61448 | tf_op jit(solution)/shard_map/ppermute | solution.py:14
  95.4 2.5 %collective-permute-start.11 = (bf16[5,16,128]{2,1,0:T(8,128)(2,1)S(1)}, bf16[5,16,128]{2,1,0:T(8,128)(2,1)S(1)}, u32[]{:S(2)}, u32[]{:S(2)}) collective-permute-start(bf16[5,16,128]{2,1,0:T(8,128)(2,1)S(1)} %slice.459), channel_id=1, source_target_pairs={{0,1},{1,2},{2,3},{3,4},{4,5},{5,6},{6,7},{7,8},{8,9},{9,10},{10,1... | collective-permute-start | bytes 61448 | tf_op jit(solution)/shard_map/ppermute | solution.py:14
  97.9 4.6 %collective-permute-done.10 = bf16[5,16,128]{2,1,0:T(8,128)(2,1)S(1)} collective-permute-done((bf16[5,16,128]{2,1,0:T(8,128)(2,1)S(1)}, bf16[5,16,128]{2,1,0:T(8,128)(2,1)S(1)}, u32[]{:S(2)}, u32[]{:S(2)}) %collective-permute-start.10) | collective-permute-done | bytes 20512 | tf_op jit(solution)/shard_map/ppermute | solution.py:14
  102.5 3.3 %collective-permute-done.11 = bf16[5,16,128]{2,1,0:T(8,128)(2,1)S(1)} collective-permute-done((bf16[5,16,128]{2,1,0:T(8,128)(2,1)S(1)}, bf16[5,16,128]{2,1,0:T(8,128)(2,1)S(1)}, u32[]{:S(2)}, u32[]{:S(2)}) %collective-permute-start.11) | collective-permute-done | bytes 20512 | tf_op jit(solution)/shard_map/ppermute | solution.py:14
  105.9 0.1 slice.322
  106.0 1.5 %reduce_window_sum.11 = f32[5,80,128]{2,1,0:T(8,128)S(1)} reduce-window(f32[5,80,128]{2,1,0:T(8,128)S(1)} %slice_dynamic-update-slice_fusion, f32[]{:T(128)} %constant.83.clone.1), window={size=1x1x128 pad=0_0x0_0x127_0}, to_apply=%region_0.1 | reduce-window | flops 6502400 | bytes 409604 | tf_op jit(solution)/shard_map/jit(cumsum)/reduce_window_sum | solution.py:216
  107.6 0.2 copy.90
  107.8 0.1 slice_reduce_fusion
  107.9 0.1 slice_subtract_fusion
  108.1 0.2 copy.72
  108.2 0.5 divide_bitcast_fusion
  108.7 0.5 fusion.81
  109.3 0.6 copy.74
  (74 shorter events, 1.4 us)
Async XLA Ops:
  0.6 5.3 %copy-start = (bf16[96,8192]{1,0:T(8,128)(2,1)S(1)}, bf16[96,8192]{1,0:T(8,128)(2,1)}, u32[]{:S(2)}) copy-start(bf16[96,8192]{1,0:T(8,128)(2,1)} %param.12) | copy-start | bytes 4718596
  5.9 12.5 %copy-start.6 = (s32[256]{0:T(256)S(1)}, s32[256]{0:T(256)}, u32[]{:S(2)}) copy-start(s32[256]{0:T(256)} %param.11) | copy-start | bytes 3076
  5.9 14.4 %copy-start.5 = (bf16[6,96,48]{1,2,0:T(8,128)(2,1)S(1)}, bf16[6,96,48]{1,2,0:T(8,128)(2,1)}, u32[]{:S(2)}) copy-start(bf16[6,96,48]{1,2,0:T(8,128)(2,1)} %param.14) | copy-start | bytes 165892
  5.9 14.4 %copy-start.8 = (bf16[6,48,288]{2,1,0:T(8,128)(2,1)S(1)}, bf16[6,48,288]{2,1,0:T(8,128)(2,1)}, u32[]{:S(2)}) copy-start(bf16[6,48,288]{2,1,0:T(8,128)(2,1)} %param.13) | copy-start | bytes 497668
  8.1 10.8 %collective-permute-start = (bf16[96,64]{0,1:T(8,128)(2,1)S(1)}, bf16[96,64]{0,1:T(8,128)(2,1)S(1)}, u32[]{:S(2)}, u32[]{:S(2)}) collective-permute-start(bf16[96,64]{0,1:T(8,128)(2,1)S(1)} %fusion.79), channel_id=1, source_target_pairs={{4,0},{8,4},{12,8},{16,12},{20,16},{24,20},{28,24},{32,28},{36,32}... | collective-permute-start | bytes 36872 | tf_op jit(solution)/shard_map/ppermute | solution.py:14
  12.0 6.9 %collective-permute-start.1 = (bf16[96,64]{0,1:T(8,128)(2,1)S(1)}, bf16[96,64]{0,1:T(8,128)(2,1)S(1)}, u32[]{:S(2)}, u32[]{:S(2)}) collective-permute-start(bf16[96,64]{0,1:T(8,128)(2,1)S(1)} %fusion.79), channel_id=1, source_target_pairs={{8,0},{12,4},{16,8},{20,12},{24,16},{28,20},{32,24},{36,28},{40,32... | collective-permute-start | bytes 36872 | tf_op jit(solution)/shard_map/ppermute | solution.py:14
  15.2 5.1 %collective-permute-start.2 = (bf16[96,64]{0,1:T(8,128)(2,1)S(1)}, bf16[96,64]{0,1:T(8,128)(2,1)S(1)}, u32[]{:S(2)}, u32[]{:S(2)}) collective-permute-start(bf16[96,64]{0,1:T(8,128)(2,1)S(1)} %fusion.79), channel_id=1, source_target_pairs={{12,0},{16,4},{20,8},{24,12},{28,16},{32,20},{36,24},{40,28},{44,3... | collective-permute-start | bytes 36872 | tf_op jit(solution)/shard_map/ppermute | solution.py:14
  20.3 2.9 %copy-start.3 = (bf16[96,96]{1,0:T(8,128)(2,1)S(1)}, bf16[96,96]{1,0:T(8,128)(2,1)}, u32[]{:S(2)}) copy-start(bf16[96,96]{1,0:T(8,128)(2,1)} %param.15) | copy-start | bytes 55300
  20.9 3.2 %copy-start.7 = (f32[48]{0:T(128)S(1)}, f32[48]{0:T(128)}, u32[]{:S(2)}) copy-start(f32[48]{0:T(128)} %param.16) | copy-start | bytes 580
  25.3 5.1 %copy-start.9 = (bf16[2,3,48,144]{3,2,1,0:T(8,128)(2,1)S(1)}, bf16[2,3,48,144]{3,2,1,0:T(8,128)(2,1)}, u32[]{:S(2)}) copy-start(bf16[2,3,48,144]{3,2,1,0:T(8,128)(2,1)} %param.17) | copy-start | bytes 248836
  32.6 2.2 %copy-start.10 = (bf16[2,48,48]{2,1,0:T(8,128)(2,1)S(1)}, bf16[2,48,48]{2,1,0:T(8,128)(2,1)}, u32[]{:S(2)}) copy-start(bf16[2,48,48]{2,1,0:T(8,128)(2,1)} %param.18) | copy-start | bytes 27652
  41.0 8.2 %collective-permute-start.3 = (bf16[48,4,1,256]{3,0,2,1:T(8,128)(2,1)S(1)}, bf16[48,4,1,256]{3,0,2,1:T(8,128)(2,1)S(1)}, u32[]{:S(2)}, u32[]{:S(2)}) collective-permute-start(bf16[48,4,1,256]{3,0,2,1:T(8,128)(2,1)S(1)} %get-tuple-element.25), channel_id=1, source_target_pairs={{0,1},{1,2},{2,3},{3,0},{4,5},{5,6},{6,7},{7,4},{8,9},{9,10},{10,1... | collective-permute-start | bytes 294920 | tf_op jit(solution)/shard_map/ppermute | solution.py:23
  44.4 6.7 %collective-permute-start.4 = (bf16[48,4,1,256]{3,0,2,1:T(8,128)(2,1)S(1)}, bf16[48,4,1,256]{3,0,2,1:T(8,128)(2,1)S(1)}, u32[]{:S(2)}, u32[]{:S(2)}) collective-permute-start(bf16[48,4,1,256]{3,0,2,1:T(8,128)(2,1)S(1)} %get-tuple-element.26), channel_id=1, source_target_pairs={{1,0},{2,1},{3,2},{0,3},{5,4},{6,5},{7,6},{4,7},{9,8},{10,9},{11,1... | collective-permute-start | bytes 294920 | tf_op jit(solution)/shard_map/ppermute | solution.py:26
  61.3 6.4 %copy-start.4 = (bf16[5,48]{1,0:T(8,128)(2,1)S(1)}, bf16[5,48]{1,0:T(8,128)(2,1)}, u32[]{:S(2)}) copy-start(bf16[5,48]{1,0:T(8,128)(2,1)} %param.19) | copy-start | bytes 1444
  69.9 10.1 %collective-permute-start.5 = (bf16[5,16,256]{2,1,0:T(8,128)(2,1)S(1)}, bf16[5,16,256]{2,1,0:T(8,128)(2,1)S(1)}, u32[]{:S(2)}, u32[]{:S(2)}) collective-permute-start(bf16[5,16,256]{2,1,0:T(8,128)(2,1)S(1)} %fusion.142), channel_id=1, source_target_pairs={{0,4},{4,8},{8,12},{12,16},{16,20},{20,24},{24,28},{28,32},{32,36}... | collective-permute-start | bytes 122888 | tf_op jit(solution)/shard_map/ppermute | solution.py:14
  72.2 9.2 %collective-permute-start.6 = (bf16[5,16,256]{2,1,0:T(8,128)(2,1)S(1)}, bf16[5,16,256]{2,1,0:T(8,128)(2,1)S(1)}, u32[]{:S(2)}, u32[]{:S(2)}) collective-permute-start(bf16[5,16,256]{2,1,0:T(8,128)(2,1)S(1)} %fusion.141), channel_id=1, source_target_pairs={{0,8},{4,12},{8,16},{12,20},{16,24},{20,28},{24,32},{28,36},{32,40... | collective-permute-start | bytes 122888 | tf_op jit(solution)/shard_map/ppermute | solution.py:14
  75.0 9.6 %collective-permute-start.7 = (bf16[5,16,256]{2,1,0:T(8,128)(2,1)S(1)}, bf16[5,16,256]{2,1,0:T(8,128)(2,1)S(1)}, u32[]{:S(2)}, u32[]{:S(2)}) collective-permute-start(bf16[5,16,256]{2,1,0:T(8,128)(2,1)S(1)} %fusion.140), channel_id=1, source_target_pairs={{0,12},{4,16},{8,20},{12,24},{16,28},{20,32},{24,36},{28,40},{32,4... | collective-permute-start | bytes 122888 | tf_op jit(solution)/shard_map/ppermute | solution.py:14
  79.7 30.2 %copy-start.1 = (bf16[96,8192]{1,0:T(8,128)(2,1)S(1)}, bf16[96,8192]{1,0:T(8,128)(2,1)}, u32[]{:S(2)}) copy-start(bf16[96,8192]{1,0:T(8,128)(2,1)} %param.12) | copy-start | bytes 4718596
  84.7 25.2 %copy-start.2 = (f32[5,16,256]{2,1,0:T(8,128)}, f32[5,16,256]{2,1,0:T(8,128)S(1)}, u32[]{:S(2)}) copy-start(f32[5,16,256]{2,1,0:T(8,128)S(1)} %fusion.146) | copy-start | bytes 245764
  84.8 13.1 %collective-permute-start.8 = (bf16[5,16,128]{2,1,0:T(8,128)(2,1)S(1)}, bf16[5,16,128]{2,1,0:T(8,128)(2,1)S(1)}, u32[]{:S(2)}, u32[]{:S(2)}) collective-permute-start(bf16[5,16,128]{2,1,0:T(8,128)(2,1)S(1)} %slice.459), channel_id=1, source_target_pairs={{0,4},{1,5},{2,6},{3,7},{4,8},{5,9},{6,10},{7,11},{8,12},{9,13},{1... | collective-permute-start | bytes 61448 | tf_op jit(solution)/shard_map/ppermute | solution.py:14
  86.8 11.1 %collective-permute-start.9 = (bf16[5,16,128]{2,1,0:T(8,128)(2,1)S(1)}, bf16[5,16,128]{2,1,0:T(8,128)(2,1)S(1)}, u32[]{:S(2)}, u32[]{:S(2)}) collective-permute-start(bf16[5,16,128]{2,1,0:T(8,128)(2,1)S(1)} %slice.459), channel_id=1, source_target_pairs={{0,3},{1,4},{2,5},{3,6},{4,7},{5,8},{6,9},{7,10},{8,11},{9,12},{10... | collective-permute-start | bytes 61448 | tf_op jit(solution)/shard_map/ppermute | solution.py:14
  91.7 10.8 %collective-permute-start.10 = (bf16[5,16,128]{2,1,0:T(8,128)(2,1)S(1)}, bf16[5,16,128]{2,1,0:T(8,128)(2,1)S(1)}, u32[]{:S(2)}, u32[]{:S(2)}) collective-permute-start(bf16[5,16,128]{2,1,0:T(8,128)(2,1)S(1)} %slice.459), channel_id=1, source_target_pairs={{0,2},{1,3},{2,4},{3,5},{4,6},{5,7},{6,8},{7,9},{8,10},{9,11},{10,... | collective-permute-start | bytes 61448 | tf_op jit(solution)/shard_map/ppermute | solution.py:14
  95.4 10.5 %collective-permute-start.11 = (bf16[5,16,128]{2,1,0:T(8,128)(2,1)S(1)}, bf16[5,16,128]{2,1,0:T(8,128)(2,1)S(1)}, u32[]{:S(2)}, u32[]{:S(2)}) collective-permute-start(bf16[5,16,128]{2,1,0:T(8,128)(2,1)S(1)} %slice.459), channel_id=1, source_target_pairs={{0,1},{1,2},{2,3},{3,4},{4,5},{5,6},{6,7},{7,8},{8,9},{9,10},{10,1... | collective-permute-start | bytes 61448 | tf_op jit(solution)/shard_map/ppermute | solution.py:14
where the time goes:
time: 110 us
  starting transfers between devices  39.4 us (36%)
  matrix products  29.1 us (26%)
  local copies, waits for them, and re-layouts  17.5 us (16%)
  waiting for transfers between devices  16.9 us (15%)
  other arithmetic  5.62 us (5%)
  between operations  1.4 us (1%)
    ppermute x10, starting transfers between devices, from_behind(): return lax.ppermute(block, axis, route)  32.2 us
    ppermute x10, waiting for transfers between devices, from_behind(): return lax.ppermute(block, axis, route)  14 us
    dot_general x2, matrix products, per_device(): jnp.einsum('oc,ckrj->okrj', tower_mix[layer_index], squeezed, preferred_e...  12.6 us
    slice x2, local copies, waits for them, and re-layouts, conv_rows(): padded[:, :, row_tap:row_tap + height, col_tap:col_tap + extent]  9.1 us
    dot_general x4, matrix products, conv_rows(): jnp.einsum('oc,ckrj->okrj', kernel[row_tap], stacked, preferred_element_t...  8.65 us
    eq x5, local copies, waits for them, and re-layouts, stem_features(): letters[:, :, None] == jnp.arange(4, dtype=jnp.int32)[None, None, :]  5.23 us
    ppermute x1, starting transfers between devices, padded_2(): lax.ppermute(lax.slice_in_dim(block, 0, width, axis=dim), axis, backward)  3.83 us
    ppermute x1, starting transfers between devices, padded_2(): lax.ppermute(lax.slice_in_dim(block, block.shape[dim] - width, None, axis...  3.4 us
  transfers between devices with their start and end apart: 12, of which 7 were waited for; matrix products, arithmetic and copies ran while one was open for 1% of the time, Pallas kernels for 0%

commit v1 on v0

v1 whole, which is shorter than its diff:
```python
import functools

import jax
import jax.numpy as jnp
from jax import lax
from jax.experimental import pallas as pl
from jax.experimental.pallas import tpu as pltpu
from jax.sharding import PartitionSpec as P

BP = 2048
STRIDE = 64
BINS = 256
BLOCKS = 4
C1 = 96
MID = 48
C2 = 48
TARGETS = 5
TRUNK = 6
HEIGHT = 16
F32 = jnp.float32
BF16 = jnp.bfloat16
CHUNKS = 4


def iota(shape, dim):
    return lax.broadcasted_iota(jnp.int32, shape, dim)


def dot(a, b):
    return jnp.dot(a, b, preferred_element_type=F32)


def shifted(value, first, last):
    width = value.shape[1]
    lane = iota(value.shape, 1)
    zero = jnp.zeros_like(value)
    before = pltpu.roll(value, 1, 1)
    after = pltpu.roll(value, width - 1, 1)
    if first:
        before = jnp.where(lane == 0, zero, before)
    if last:
        after = jnp.where(lane == width - 1, zero, after)
    return before, after


def skewed(value, sign):
    width = value.shape[2]
    row = iota(value.shape, 1)
    for bit in (1, 2, 4, 8):
        turned = pltpu.roll(value, bit if sign > 0 else width - bit, 2)
        value = jnp.where(jnp.bitwise_and(row, bit) != 0, turned, value)
    return value


def kernel(
    genomes,
    towers,
    bases_hbm,
    stitch_hbm,
    stem_hbm,
    trunk_in_hbm,
    trunk_out_hbm,
    pair_hbm,
    rate_hbm,
    conv_hbm,
    mix_hbm,
    head_hbm,
    band_hbm,
    scores_hbm,
    bases,
    stitch,
    stem,
    trunk_in,
    trunk_out,
    pair,
    rate,
    conv,
    mix,
    head,
    onehot,
    window,
    taps,
    wide_conv,
    wide_mix,
    wide_head,
    decay,
    rates,
    row_weights,
    left,
    right,
    x1,
    x2,
    grid1,
    final,
    sent,
    landed,
    own_piece,
    band,
    part,
    parts_in,
    scores,
    in_sems,
    stem_sems,
    out_sems,
    feature_send,
    feature_recv,
    piece_send,
    piece_recv,
    part_send,
    part_recv,
):
    g = lax.axis_index("genome")
    t = lax.axis_index("tower")

    def at_genome(step):
        return {"genome": lax.rem(g + step + genomes, genomes), "tower": t}

    def at_band(step):
        place = t + step + towers
        up = lax.div(place, towers) - 1
        return {"genome": lax.rem(g + up + genomes, genomes), "tower": lax.rem(place, towers)}

    barrier = pltpu.get_barrier_semaphore()
    peers = [at_genome(s) for s in (-1, 1, -2, 2, -3, 3)] + [at_band(s) for s in (-1, 1, -2, 2, -3, 3)]
    for peer in peers:
        pl.semaphore_signal(barrier, inc=1, device_id=peer, device_id_type=pl.DeviceIdType.MESH)

    chunk = 4 * BP // CHUNKS
    bases_copy = pltpu.make_async_copy(bases_hbm, bases, in_sems.at[0])
    bases_copy.start()
    stem_copies = []
    for k in range(CHUNKS):
        lanes = pl.ds(k * chunk, chunk)
        stem_copies.append(pltpu.make_async_copy(stem_hbm.at[:, lanes], stem.at[:, lanes], stem_sems.at[k]))
        stem_copies[-1].start()
    small = [
        (stitch_hbm, stitch),
        (trunk_in_hbm, trunk_in),
        (trunk_out_hbm, trunk_out),
        (pair_hbm, pair),
        (rate_hbm, rate),
        (conv_hbm, conv),
        (mix_hbm, mix),
        (head_hbm, head),
    ]
    small_copies = [pltpu.make_async_copy(a, b, in_sems.at[i + 1]) for i, (a, b) in enumerate(small)]
    for copy in small_copies:
        copy.start()

    bases_copy.wait()
    spread = jnp.where(lax.shift_right_logical(iota((128, 512), 1), 2) == iota((128, 512), 0), 1.0, 0.0).astype(BF16)
    letter = jnp.bitwise_and(iota((STRIDE, 512), 1), 3).astype(F32)
    summed = jnp.zeros((STRIDE, C1), F32)
    for k in range(CHUNKS):
        for q in range(16 // CHUNKS):
            rows = bases[pl.ds(k * (16 // CHUNKS) + q, STRIDE, stride=16), :]
            repeated = dot(rows.astype(F32).astype(BF16), spread)
            onehot[:, pl.ds(q * 512, 512)] = jnp.where(repeated == letter, 1.0, 0.0).astype(BF16)
        stem_copies[k].wait()
        summed = summed + lax.dot_general(
            onehot[...], stem[:, pl.ds(k * chunk, chunk)], (((1,), (1,)), ((), ())), preferred_element_type=F32
        )
    window[0] = jnp.concatenate([summed, jnp.zeros((STRIDE, 128 - C1), F32)], axis=1).astype(BF16)

    pl.semaphore_wait(barrier, len(peers))
    feature_copies = []
    for s in range(1, BLOCKS):
        feature_copies.append(
            pltpu.make_async_remote_copy(
                src_ref=window.at[0],
                dst_ref=window.at[s],
                send_sem=feature_send.at[s - 1],
                recv_sem=feature_recv.at[s - 1],
                device_id=at_genome(-s),
                device_id_type=pl.DeviceIdType.MESH,
            )
        )
        feature_copies[-1].start()

    for copy in small_copies:
        copy.wait()
    for l in range(TRUNK):
        for q in range(3):
            taps[l, pl.ds(q * MID, MID), :] = trunk_in[l, :, pl.ds(q * C1, C1)]
    for l in range(2):
        for o in range(3):
            parts = []
            if o:
                parts.append(jnp.zeros((C2, 144 * o), BF16))
            parts += [conv[l, u] for u in range(3)]
            if o < 2:
                parts.append(jnp.zeros((C2, 144 * (2 - o)), BF16))
            wide_conv[l, pl.ds(o * C2, C2), :] = jnp.concatenate(parts, axis=1)
            parts = []
            if o:
                parts.append(jnp.zeros((C2, C2 * o), BF16))
            parts.append(mix[l])
            if o < 2:
                parts.append(jnp.zeros((C2, C2 * (2 - o)), BF16))
            wide_mix[l, pl.ds(o * C2, C2), :] = jnp.concatenate(parts, axis=1)
    lane = iota((C2, HEIGHT * C2), 1)
    row_of = lax.shift_right_logical(lane * 1366, 16)
    tile = jnp.where(lane - row_of * C2 == iota((C2, HEIGHT * C2), 0), 1.0, 0.0).astype(BF16)
    head_rows = jnp.concatenate(
        [jnp.broadcast_to(head[k : k + 1].astype(F32), (HEIGHT, C2)) for k in range(TARGETS)], axis=0
    ).astype(BF16)
    many = (TARGETS * HEIGHT, HEIGHT * C2)
    row_of = lax.shift_right_logical(iota(many, 1) * 1366, 16)
    wide_head[...] = jnp.where(
        row_of == jnp.bitwise_and(iota(many, 0), HEIGHT - 1), dot(head_rows, tile), 0.0
    ).astype(BF16)
    first_row = HEIGHT * t
    for b in range(BLOCKS):
        rows = STRIDE * b - 2 + first_row + iota((24, BINS), 0)
        gap = jnp.abs(rows - iota((24, BINS), 1)).astype(F32)
        decay[b] = jnp.log(1.0 + gap)
    square = (C2, C2)
    column = jnp.sum(
        jnp.where(iota(square, 0) == iota(square, 1), jnp.broadcast_to(rate[...], square), 0.0), axis=1, keepdims=True
    )
    rates[...] = jnp.broadcast_to(column, (C2, 128))
    band_shape = (HEIGHT, BINS)
    weights = jnp.broadcast_to(stitch[...].astype(F32), band_shape)
    lane = iota(band_shape, 1)
    row = iota(band_shape, 0)
    total = jnp.zeros(band_shape, F32)
    for b in range(BLOCKS):
        place = STRIDE * b + first_row + row
        column = jnp.sum(jnp.where(lane == place, weights, 0.0), axis=1, keepdims=True)
        column = jnp.broadcast_to(column, band_shape)
        inside = lane + place < BINS
        row_weights[b] = jnp.where(inside, column, 0.0)
        total = total + jnp.where(jnp.logical_and(inside, g >= b), column, 0.0)
    row_weights[BLOCKS] = 1.0 / jnp.maximum(total, 1.0)

    for copy in feature_copies:
        copy.wait_recv()
    slots = [window[0].astype(F32)]
    for s in range(1, BLOCKS):
        slots.append(jnp.where(g + s < genomes, window[s].astype(F32), 0.0))
    stream = jnp.concatenate(slots, axis=0).T[:C1]
    lane = iota((MID, BINS), 1)
    for l in range(TRUNK):
        dilation = max(1, BINS // 2 ** (TRUNK - l))
        taken = dot(taps[l], jnp.maximum(stream, 0.0).astype(BF16))
        before = jnp.where(lane >= dilation, pltpu.roll(taken[:MID], dilation, 1), 0.0)
        after = jnp.where(lane < BINS - dilation, pltpu.roll(taken[2 * MID :], BINS - dilation, 1), 0.0)
        squeezed = jnp.maximum(before + taken[MID : 2 * MID] + after, 0.0).astype(BF16)
        stream = stream + dot(trunk_out[l], squeezed)
    projected = dot(pair[...], jnp.maximum(stream, 0.0).astype(BF16))
    left[...] = pltpu.roll(projected[:C2], lax.rem(2 - first_row + BINS, BINS), 1)
    right[...] = projected[C2:]

    piece_copies = []
    for b in range(BLOCKS - 1, -1, -1):
        lo = 128 if b == 3 else 0
        width = BINS - lo
        lanes = pl.ds(lo, width)
        first = lo == 0

        def put(ref, at, value):
            before, after = shifted(value, first, True)
            ref[pl.ds(at, C2), lanes] = before
            ref[pl.ds(at + C2, C2), lanes] = value
            ref[pl.ds(at + 2 * C2, C2), lanes] = after

        base = STRIDE * b - 2 + first_row
        decline = jnp.concatenate([rates[...]] * (width // 128), axis=1)
        for r in range(HEIGHT + 4):
            at = STRIDE * b + r
            mixed = (
                jnp.broadcast_to(left[:, at : at + 1], (C2, width))
                + right[:, lanes]
                - decline * jnp.broadcast_to(decay[b, r : r + 1, lanes], (C2, width))
            )
            mixed = jnp.maximum(mixed, 0.0)
            if (b == 0 and r < 2) or (b == BLOCKS - 1 and r >= HEIGHT + 2):
                mixed = jnp.where(jnp.logical_and(base + r >= 0, base + r < BINS), mixed, 0.0)
            put(x1, 144 * r, mixed.astype(BF16))

        for k in range(6):
            convolved = dot(wide_conv[0], x1[pl.ds(432 * k, 720), lanes])
            mixed = dot(wide_mix[0], jnp.maximum(convolved, 0.0).astype(BF16))
            for o in range(3):
                r = 3 * k + o + 1
                held = x1[pl.ds(144 * r + C2, C2), lanes].astype(F32)
                value = held + mixed[o * C2 : (o + 1) * C2]
                grid1[pl.ds(C2 * (r - 1), C2), lanes] = value
                value = jnp.maximum(value, 0.0)
                if (b == 0 and r < 2) or (b == BLOCKS - 1 and r >= HEIGHT + 2):
                    value = jnp.where(jnp.logical_and(base + r >= 0, base + r < BINS), value, 0.0)
                put(x2, 144 * (r - 1), value.astype(BF16))

        for k in range(6):
            r0 = min(3 * k, HEIGHT - 3)
            convolved = dot(wide_conv[1], x2[pl.ds(144 * r0, 720), lanes])
            mixed = dot(wide_mix[1], jnp.maximum(convolved, 0.0).astype(BF16))
            value = grid1[pl.ds(C2 * (r0 + 1), 144), lanes] + mixed
            final[pl.ds(C2 * r0, 144), lanes] = jnp.maximum(value, 0.0).astype(BF16)

        contact = dot(wide_head[...], final[:, lanes])
        if lo:
            contact = jnp.concatenate([jnp.zeros((TARGETS * HEIGHT, lo), F32), contact], axis=1)
        contact = contact.reshape(TARGETS, HEIGHT, BINS)
        turn = lax.rem(2 * BINS - STRIDE * b - first_row, BINS)
        piece = skewed(pltpu.roll(contact, turn, 2), -1) * row_weights[b][None]
        if b == 0:
            own_piece[...] = piece
        else:
            span = BINS if b == 1 else 128
            sent[b - 1] = piece.astype(BF16)
            copy = pltpu.make_async_remote_copy(
                src_ref=sent.at[b - 1, :, :, pl.ds(0, span)],
                dst_ref=landed.at[b - 1, :, :, pl.ds(0, span)],
                send_sem=piece_send.at[b - 1],
                recv_sem=piece_recv.at[b - 1],
                device_id=at_genome(b),
                device_id_type=pl.DeviceIdType.MESH,
            )
            copy.start()
            piece_copies.append(copy)

    for copy in piece_copies:
        copy.wait_recv()
    near = own_piece[:, :, :128]
    for b in range(1, BLOCKS):
        near = near + jnp.where(g >= b, landed[b - 1, :, :, :128].astype(F32), 0.0)
    far = own_piece[:, :, 128:] + jnp.where(g >= 1, landed[0, :, :, 128:].astype(F32), 0.0)
    near = near * row_weights[BLOCKS, :, :128][None]
    band[:, :, :128] = near
    band[:, :, 128:] = far * row_weights[BLOCKS, :, 128:][None]
    band_copy = pltpu.make_async_copy(band, band_hbm, out_sems.at[0])
    band_copy.start()

    shape = (TARGETS, HEIGHT, 128)
    lane = iota(shape, 2)
    run = near
    for step in (1, 2, 4, 8, 16, 32):
        run = run + pltpu.roll(run, 128 - step, 2)
    inside = jnp.where(jnp.logical_and(lane >= 1, lane <= STRIDE), run, 0.0)
    insulation = jnp.sum(skewed(pltpu.roll(inside, 127, 2), 1), axis=1)
    contact = jnp.where(jnp.logical_and(lane >= 1, lane <= STRIDE), jnp.exp(near), 0.0)
    upstream = jnp.sum(skewed(contact, 1), axis=1)
    downstream = jnp.sum(contact, axis=2, keepdims=True)
    downstream = jnp.sum(jnp.where(lane == iota(shape, 1), jnp.broadcast_to(downstream, shape), 0.0), axis=1)
    part[0:TARGETS] = insulation
    part[8 : 8 + TARGETS] = upstream
    part_copies = []
    for m in range(1, BLOCKS + 1):
        copy = pltpu.make_async_remote_copy(
            src_ref=part,
            dst_ref=parts_in.at[m - 1],
            send_sem=part_send.at[m - 1],
            recv_sem=part_recv.at[m - 1],
            device_id=at_band(m),
            device_id_type=pl.DeviceIdType.MESH,
        )
        copy.start()
        part_copies.append(copy)
    for copy in part_copies:
        copy.wait_recv()
    place = g * towers + t
    flat = (TARGETS, 128)
    lane = iota(flat, 1)
    for m in range(1, BLOCKS + 1):
        turn = 128 - HEIGHT * m
        absent = float(HEIGHT) if m < BLOCKS else (HEIGHT - lane).astype(F32)
        insulation = insulation + jnp.where(place >= m, pltpu.roll(parts_in[m - 1, 0:TARGETS], turn, 1), 0.0)
        upstream = upstream + jnp.where(place >= m, pltpu.roll(parts_in[m - 1, 8 : 8 + TARGETS], turn, 1), absent)
    scores[0] = (insulation * (1.0 / (STRIDE * STRIDE)))[:, :HEIGHT]
    scores[1] = ((downstream - upstream) / (downstream + upstream))[:, :HEIGHT]
    scores_copy = pltpu.make_async_copy(scores, scores_hbm, out_sems.at[1])
    scores_copy.start()
    for copy in feature_copies + piece_copies + part_copies:
        copy.wait_send()
    band_copy.wait()
    scores_copy.wait()


def solution(mesh):
    genomes, towers = mesh.shape["genome"], mesh.shape["tower"]

    def per_device(bases, stitch, stem, trunk_in, trunk_out, pair, rate, conv, mix, head):
        anywhere = pl.BlockSpec(memory_space=pl.ANY)
        vmem = pltpu.VMEM
        dma = pltpu.SemaphoreType.DMA
        many = TARGETS * HEIGHT
        return pl.pallas_call(
            functools.partial(kernel, genomes, towers),
            out_shape=(
                jax.ShapeDtypeStruct((TARGETS, HEIGHT, BINS), F32),
                jax.ShapeDtypeStruct((2, TARGETS, HEIGHT), F32),
            ),
            in_specs=[anywhere] * 10,
            out_specs=(anywhere, anywhere),
            scratch_shapes=[
                vmem((1024, 128), jnp.int32),
                vmem((1, BINS), jnp.int32),
                vmem((C1, 4 * BP), BF16),
                vmem((TRUNK, MID, 3 * C1), BF16),
                vmem((TRUNK, C1, MID), BF16),
                vmem((2 * C2, C1), BF16),
                vmem((1, C2), F32),
                vmem((2, 3, C2, 3 * C2), BF16),
                vmem((2, C2, C2), BF16),
                vmem((TARGETS, C2), BF16),
                vmem((STRIDE, 4 * BP // CHUNKS), BF16),
                vmem((BLOCKS, STRIDE, 128), BF16),
                vmem((TRUNK, 3 * MID, C1), BF16),
                vmem((2, 3 * C2, 15 * C2), BF16),
                vmem((2, 3 * C2, 3 * C2), BF16),
                vmem((many, HEIGHT * C2), BF16),
                vmem((BLOCKS, 24, BINS), F32),
                vmem((C2, 128), F32),
                vmem((BLOCKS + 1, HEIGHT, BINS), F32),
                vmem((C2, BINS), F32),
                vmem((C2, BINS), F32),
                vmem((20 * 144, BINS), BF16),
                vmem((18 * 144, BINS), BF16),
                vmem((18 * C2, BINS), F32),
                vmem((HEIGHT * C2, BINS), BF16),
                vmem((BLOCKS - 1, TARGETS, HEIGHT, BINS), BF16),
                vmem((BLOCKS - 1, TARGETS, HEIGHT, BINS), BF16),
                vmem((TARGETS, HEIGHT, BINS), F32),
                vmem((TARGETS, HEIGHT, BINS), F32),
                vmem((16, 128), F32),
                vmem((BLOCKS, 16, 128), F32),
                vmem((2, TARGETS, HEIGHT), F32),
                dma((9,)),
                dma((CHUNKS,)),
                dma((2,)),
                dma((BLOCKS - 1,)),
                dma((BLOCKS - 1,)),
                dma((BLOCKS - 1,)),
                dma((BLOCKS - 1,)),
                dma((BLOCKS,)),
                dma((BLOCKS,)),
            ],
            compiler_params=pltpu.CompilerParams(collective_id=0, has_side_effects=True),
            name="contacts",
        )(
            bases.reshape(-1, 128),
            stitch.reshape(1, -1),
            stem,
            trunk_in,
            trunk_out,
            pair,
            rate.reshape(1, -1),
            conv,
            mix,
            head,
        )

    placed = (P("genome"), P(), P(), P(), P(), P(), P(), P(), P(), P())
    return jax.shard_map(
        per_device,
        mesh=mesh,
        in_specs=placed,
        out_specs=(P(None, ("genome", "tower"), None), P(None, None, ("genome", "tower"))),
        check_vma=False,
    )
```

time: 110 us -> 48.5 us (0.44)
  the two profiles are of different devices: /device:TPU:256 before, /device:TPU:1 now
where the time goes in v1:
time: 48.5 us; the launch traced here: 48.2 us
  Pallas kernels  43.1 us (89%)
  local copies, waits for them, and re-layouts  4.48 us (9%)
  between operations  0.64 us (1%)
    pallas_call x1, Pallas kernels, per_device(): pl.pallas_call(functools.partial(kernel, genomes, towers), out_shape=(jax...  43.1 us
    unnamed x2, local copies, waits for them, and re-layouts  3.18 us
    pallas_call x1, local copies, waits for them, and re-layouts, per_device(): pl.pallas_call(functools.partial(kernel, genomes, towers), out_shape=(jax...  1.29 us

profile of v1, /device:TPU:1, one launch (start us, length us, event | category | flops | bytes accessed | tf_op | source)
XLA Modules:
  0.0 48.2 jit_solution(8664581129592860185)
XLA Ops:
  0.6 1.7 %copy.12.trunk_out_hbm = bf16[6,96,48]{2,1,0:T(8,128)(2,1)} copy(bf16[6,96,48]{1,2,0:T(8,128)(2,1)} %param.14) | data formatting | bytes 110592 | tf_op args[4]
  2.3 43.1 %contacts.1 = (f32[5,16,256]{2,1,0:T(8,128)}, f32[2,5,16]{2,1,0:T(8,128)}) custom-call(s32[1024,128]{1,0:T(8,128)} %bitcast.3, s32[1,256]{1,0:T(1,128)} %bitcast.4, bf16[96,8192]{1,0:T(8,128)(2,1)} %stem_hbm.1, bf16[6,48,288]{2,1,0:T(8,128)(2,1)} %trunk_in_hbm.1, bf16[6,96,48]{2,1,0:T(8,128)(2,1)} %copy.12.trunk_out_hbm, bf16[96,96]{1,0:T(8,128)(2,1)} %pair_hbm.1, ...), custom_call_target="tpu_custom_call" | custom-call | tf_op jit(solution)/shard_map/contacts/pallas_call | solution.py:388
  45.4 1.3 %copy.13 = f32[2,5,16]{2,0,1:T(2,128)} copy(f32[2,5,16]{2,1,0:T(8,128)} %get-tuple-element.3) | data formatting | bytes 1280 | tf_op jit(solution)/shard_map/contacts/pallas_call | solution.py:388
  46.7 1.5 %copy.15 = f32[5,16,256]{2,1,0:T(8,128)} copy(f32[5,16,256]{2,1,0:T(8,128)} %get-tuple-element.6) | data formatting | bytes 163840

commit v2 on v1

--- a/solution.py
+++ b/solution.py
@@ -65,8 +65,8 @@
     conv_hbm,
     mix_hbm,
     head_hbm,
-    band_hbm,
-    scores_hbm,
+    band,
+    scores,
     bases,
     stitch,
     stem,
@@ -80,6 +80,7 @@
     onehot,
     window,
     taps,
+    widen,
     wide_conv,
     wide_mix,
     wide_head,
@@ -95,13 +96,10 @@
     sent,
     landed,
     own_piece,
-    band,
     part,
     parts_in,
-    scores,
     in_sems,
     stem_sems,
-    out_sems,
     feature_send,
     feature_recv,
     piece_send,
@@ -112,18 +110,25 @@
     g = lax.axis_index("genome")
     t = lax.axis_index("tower")
 
+    place = g * towers + t
+
     def at_genome(step):
-        return {"genome": lax.rem(g + step + genomes, genomes), "tower": t}
+        return {"genome": g + step, "tower": t}, jnp.logical_and(g + step >= 0, g + step < genomes)
 
     def at_band(step):
-        place = t + step + towers
-        up = lax.div(place, towers) - 1
-        return {"genome": lax.rem(g + up + genomes, genomes), "tower": lax.rem(place, towers)}
+        up = lax.div(t + step + towers, towers) - 1
+        near = {"genome": g + up, "tower": t + step - up * towers}
+        return near, jnp.logical_and(place + step >= 0, place + step < genomes * towers)
 
     barrier = pltpu.get_barrier_semaphore()
-    peers = [at_genome(s) for s in (-1, 1, -2, 2, -3, 3)] + [at_band(s) for s in (-1, 1, -2, 2, -3, 3)]
-    for peer in peers:
-        pl.semaphore_signal(barrier, inc=1, device_id=peer, device_id_type=pl.DeviceIdType.MESH)
+    steps = (-1, 1, -2, 2, -3, 3)
+    present = jnp.int32(0)
+    for device, there in [at_genome(s) for s in steps] + [at_band(s) for s in steps]:
+        present = present + there.astype(jnp.int32)
+
+        @pl.when(there)
+        def _():
+            pl.semaphore_signal(barrier, inc=1, device_id=device, device_id_type=pl.DeviceIdType.MESH)
 
     chunk = 4 * BP // CHUNKS
     bases_copy = pltpu.make_async_copy(bases_hbm, bases, in_sems.at[0])
@@ -162,26 +167,44 @@
         )
     window[0] = jnp.concatenate([summed, jnp.zeros((STRIDE, 128 - C1), F32)], axis=1).astype(BF16)
 
-    pl.semaphore_wait(barrier, len(peers))
+    pl.semaphore_wait(barrier, present)
+    sends = []
+
+    def send(source, target, send_sem, recv_sem, to):
+        device, there = to
+        copy = pltpu.make_async_remote_copy(
+            src_ref=source,
+            dst_ref=target,
+            send_sem=send_sem,
+            recv_sem=recv_sem,
+            device_id=device,
+            device_id_type=pl.DeviceIdType.MESH,
+        )
+
+        @pl.when(there)
+        def _():
+            copy.start()
+
+        sends.append((copy, there))
+        return copy
+
+    def receive(copy, there):
+        @pl.when(there)
+        def _():
+            copy.wait_recv()
+
     feature_copies = []
     for s in range(1, BLOCKS):
         feature_copies.append(
-            pltpu.make_async_remote_copy(
-                src_ref=window.at[0],
-                dst_ref=window.at[s],
-                send_sem=feature_send.at[s - 1],
-                recv_sem=feature_recv.at[s - 1],
-                device_id=at_genome(-s),
-                device_id_type=pl.DeviceIdType.MESH,
-            )
+            send(window.at[0], window.at[s], feature_send.at[s - 1], feature_recv.at[s - 1], at_genome(-s))
         )
-        feature_copies[-1].start()
 
     for copy in small_copies:
         copy.wait()
     for l in range(TRUNK):
         for q in range(3):
             taps[l, pl.ds(q * MID, MID), :] = trunk_in[l, :, pl.ds(q * C1, C1)]
+        widen[l] = trunk_out[l].astype(F32).T.astype(BF16)
     for l in range(2):
         for o in range(3):
             parts = []
@@ -225,16 +248,16 @@
     row = iota(band_shape, 0)
     total = jnp.zeros(band_shape, F32)
     for b in range(BLOCKS):
-        place = STRIDE * b + first_row + row
-        column = jnp.sum(jnp.where(lane == place, weights, 0.0), axis=1, keepdims=True)
+        spot = STRIDE * b + first_row + row
+        column = jnp.sum(jnp.where(lane == spot, weights, 0.0), axis=1, keepdims=True)
         column = jnp.broadcast_to(column, band_shape)
-        inside = lane + place < BINS
+        inside = lane + spot < BINS
         row_weights[b] = jnp.where(inside, column, 0.0)
         total = total + jnp.where(jnp.logical_and(inside, g >= b), column, 0.0)
     row_weights[BLOCKS] = 1.0 / jnp.maximum(total, 1.0)
 
-    for copy in feature_copies:
-        copy.wait_recv()
+    for s, copy in enumerate(feature_copies):
+        receive(copy, g + s + 1 < genomes)
     slots = [window[0].astype(F32)]
     for s in range(1, BLOCKS):
         slots.append(jnp.where(g + s < genomes, window[s].astype(F32), 0.0))
@@ -246,12 +269,12 @@
         before = jnp.where(lane >= dilation, pltpu.roll(taken[:MID], dilation, 1), 0.0)
         after = jnp.where(lane < BINS - dilation, pltpu.roll(taken[2 * MID :], BINS - dilation, 1), 0.0)
         squeezed = jnp.maximum(before + taken[MID : 2 * MID] + after, 0.0).astype(BF16)
-        stream = stream + dot(trunk_out[l], squeezed)
+        stream = stream + dot(widen[l], squeezed)
     projected = dot(pair[...], jnp.maximum(stream, 0.0).astype(BF16))
     left[...] = pltpu.roll(projected[:C2], lax.rem(2 - first_row + BINS, BINS), 1)
     right[...] = projected[C2:]
 
-    piece_copies = []
+    piece_copies = {}
     for b in range(BLOCKS - 1, -1, -1):
         lo = 128 if b == 3 else 0
         width = BINS - lo
@@ -309,19 +332,11 @@
         else:
             span = BINS if b == 1 else 128
             sent[b - 1] = piece.astype(BF16)
-            copy = pltpu.make_async_remote_copy(
-                src_ref=sent.at[b - 1, :, :, pl.ds(0, span)],
-                dst_ref=landed.at[b - 1, :, :, pl.ds(0, span)],
-                send_sem=piece_send.at[b - 1],
-                recv_sem=piece_recv.at[b - 1],
-                device_id=at_genome(b),
-                device_id_type=pl.DeviceIdType.MESH,
-            )
-            copy.start()
-            piece_copies.append(copy)
-
-    for copy in piece_copies:
-        copy.wait_recv()
+            source, target = (ref.at[b - 1, :, :, pl.ds(0, span)] for ref in (sent, landed))
+            piece_copies[b] = send(source, target, piece_send.at[b - 1], piece_recv.at[b - 1], at_genome(b))
+
+    for b, copy in piece_copies.items():
+        receive(copy, g >= b)
     near = own_piece[:, :, :128]
     for b in range(1, BLOCKS):
         near = near + jnp.where(g >= b, landed[b - 1, :, :, :128].astype(F32), 0.0)
@@ -329,8 +344,6 @@
     near = near * row_weights[BLOCKS, :, :128][None]
     band[:, :, :128] = near
     band[:, :, 128:] = far * row_weights[BLOCKS, :, 128:][None]
-    band_copy = pltpu.make_async_copy(band, band_hbm, out_sems.at[0])
-    band_copy.start()
 
     shape = (TARGETS, HEIGHT, 128)
     lane = iota(shape, 2)
@@ -345,21 +358,11 @@
     downstream = jnp.sum(jnp.where(lane == iota(shape, 1), jnp.broadcast_to(downstream, shape), 0.0), axis=1)
     part[0:TARGETS] = insulation
     part[8 : 8 + TARGETS] = upstream
-    part_copies = []
-    for m in range(1, BLOCKS + 1):
-        copy = pltpu.make_async_remote_copy(
-            src_ref=part,
-            dst_ref=parts_in.at[m - 1],
-            send_sem=part_send.at[m - 1],
-            recv_sem=part_recv.at[m - 1],
-            device_id=at_band(m),
-            device_id_type=pl.DeviceIdType.MESH,
-        )
-        copy.start()
-        part_copies.append(copy)
-    for copy in part_copies:
-        copy.wait_recv()
-    place = g * towers + t
+    part_copies = [
+        send(part, parts_in.at[m - 1], part_send.at[m - 1], part_recv.at[m - 1], at_band(m)) for m in range(1, BLOCKS + 1)
+    ]
+    for m, copy in enumerate(part_copies):
+        receive(copy, place > m)
     flat = (TARGETS, 128)
     lane = iota(flat, 1)
     for m in range(1, BLOCKS + 1):
@@ -367,14 +370,21 @@
         absent = float(HEIGHT) if m < BLOCKS else (HEIGHT - lane).astype(F32)
         insulation = insulation + jnp.where(place >= m, pltpu.roll(parts_in[m - 1, 0:TARGETS], turn, 1), 0.0)
         upstream = upstream + jnp.where(place >= m, pltpu.roll(parts_in[m - 1, 8 : 8 + TARGETS], turn, 1), absent)
-    scores[0] = (insulation * (1.0 / (STRIDE * STRIDE)))[:, :HEIGHT]
-    scores[1] = ((downstream - upstream) / (downstream + upstream))[:, :HEIGHT]
-    scores_copy = pltpu.make_async_copy(scores, scores_hbm, out_sems.at[1])
-    scores_copy.start()
-    for copy in feature_copies + piece_copies + part_copies:
-        copy.wait_send()
-    band_copy.wait()
-    scores_copy.wait()
+    scores[:, 0, :] = (insulation * (1.0 / (STRIDE * STRIDE)))[:, :HEIGHT]
+    scores[:, 1, :] = ((downstream - upstream) / (downstream + upstream))[:, :HEIGHT]
+    for copy, there in sends:
+
+        @pl.when(there)
+        def _():
+            copy.wait_send()
+
+
+def hand_over(band, scores, band_hbm, scores_hbm, sems):
+    copies = [pltpu.make_async_copy(a, b, sems.at[i]) for i, (a, b) in enumerate(((band, band_hbm), (scores, scores_hbm)))]
+    for copy in copies:
+        copy.start()
+    for copy in copies:
+        copy.wait()
 
 
 def solution(mesh):
@@ -385,20 +395,22 @@
         vmem = pltpu.VMEM
         dma = pltpu.SemaphoreType.DMA
         many = TARGETS * HEIGHT
-        return pl.pallas_call(
+        shapes = (
+            jax.ShapeDtypeStruct((TARGETS, HEIGHT, BINS), F32),
+            jax.ShapeDtypeStruct((TARGETS, 2, HEIGHT), F32),
+        )
+        in_vmem = pl.BlockSpec(memory_space=pltpu.VMEM)
+        results = pl.pallas_call(
             functools.partial(kernel, genomes, towers),
-            out_shape=(
-                jax.ShapeDtypeStruct((TARGETS, HEIGHT, BINS), F32),
-                jax.ShapeDtypeStruct((2, TARGETS, HEIGHT), F32),
-            ),
+            out_shape=shapes,
             in_specs=[anywhere] * 10,
-            out_specs=(anywhere, anywhere),
+            out_specs=(in_vmem, in_vmem),
             scratch_shapes=[
                 vmem((1024, 128), jnp.int32),
                 vmem((1, BINS), jnp.int32),
                 vmem((C1, 4 * BP), BF16),
                 vmem((TRUNK, MID, 3 * C1), BF16),
-                vmem((TRUNK, C1, MID), BF16),
+                vmem((TRUNK, MID, C1), BF16),
                 vmem((2 * C2, C1), BF16),
                 vmem((1, C2), F32),
                 vmem((2, 3, C2, 3 * C2), BF16),
@@ -407,6 +419,7 @@
                 vmem((STRIDE, 4 * BP // CHUNKS), BF16),
                 vmem((BLOCKS, STRIDE, 128), BF16),
                 vmem((TRUNK, 3 * MID, C1), BF16),
+                vmem((TRUNK, C1, MID), BF16),
                 vmem((2, 3 * C2, 15 * C2), BF16),
                 vmem((2, 3 * C2, 3 * C2), BF16),
                 vmem((many, HEIGHT * C2), BF16),
@@ -422,13 +435,10 @@
                 vmem((BLOCKS - 1, TARGETS, HEIGHT, BINS), BF16),
                 vmem((BLOCKS - 1, TARGETS, HEIGHT, BINS), BF16),
                 vmem((TARGETS, HEIGHT, BINS), F32),
-                vmem((TARGETS, HEIGHT, BINS), F32),
                 vmem((16, 128), F32),
                 vmem((BLOCKS, 16, 128), F32),
-                vmem((2, TARGETS, HEIGHT), F32),
                 dma((9,)),
                 dma((CHUNKS,)),
-                dma((2,)),
                 dma((BLOCKS - 1,)),
                 dma((BLOCKS - 1,)),
                 dma((BLOCKS - 1,)),
@@ -443,13 +453,22 @@
             stitch.reshape(1, -1),
             stem,
             trunk_in,
-            trunk_out,
+            jnp.swapaxes(trunk_out, 1, 2),
             pair,
             rate.reshape(1, -1),
             conv,
             mix,
             head,
         )
+        band, scores = pl.pallas_call(
+            hand_over,
+            out_shape=shapes,
+            in_specs=[in_vmem, in_vmem],
+            out_specs=(anywhere, anywhere),
+            scratch_shapes=[dma((2,))],
+            name="hand_over",
+        )(*results)
+        return band, jnp.swapaxes(scores, 0, 1)
 
     placed = (P("genome"), P(), P(), P(), P(), P(), P(), P(), P(), P())
     return jax.shard_map(

time: 48.5 us -> 37.4 us (0.77)
  the two profiles are of different devices: /device:TPU:1 before, /device:TPU:256 now
where the time goes in v2:
time: 37.4 us; the launch traced here: 37.2 us
  Pallas kernels  36.6 us (98%)
  between operations  0.64 us (2%)
    pallas_call x1, Pallas kernels, per_device(): pl.pallas_call(functools.partial(kernel, genomes, towers), out_shape=shap...  35 us
    pallas_call x1, Pallas kernels, per_device(): pl.pallas_call(hand_over, out_shape=shapes, in_specs=[in_vmem, in_vmem],...  1.54 us

profile of v2, /device:TPU:256, one launch (start us, length us, event | category | flops | bytes accessed | tf_op | source)
XLA Modules:
  0.0 37.2 jit_solution(2920354566875660495)
XLA Ops:
  0.6 35.0 %contacts.1 = (f32[5,16,256]{2,1,0:T(8,128)}, f32[5,2,16]{2,1,0:T(2,128)}) custom-call(s32[1024,128]{1,0:T(8,128)} %bitcast.5, s32[1,256]{1,0:T(1,128)} %bitcast.7, bf16[96,8192]{1,0:T(8,128)(2,1)} %stem_hbm.1, bf16[6,48,288]{2,1,0:T(8,128)(2,1)} %trunk_in_hbm.1, bf16[6,48,96]{2,1,0:T(8,128)(2,1)} %bitcast.6, bf16[96,96]{1,0:T(8,128)(2,1)} %pair_hbm.1, ...), custom_call_target="tpu_custom_call" | custom-call | tf_op jit(solution)/shard_map/contacts/pallas_call | solution.py:403
  35.7 1.5 %hand_over.1 = (f32[5,16,256]{2,1,0:T(8,128)}, f32[5,2,16]{2,1,0:T(2,128)}) custom-call(f32[5,16,256]{2,1,0:T(8,128)} %get-tuple-element.6.band, f32[5,2,16]{2,1,0:T(2,128)} %get-tuple-element.7.scores), custom_call_target="tpu_custom_call" | custom-call | tf_op jit(solution)/shard_map/hand_over/pallas_call | solution.py:463

commit v3 on v2

--- a/solution.py
+++ b/solution.py
@@ -20,6 +20,8 @@
 F32 = jnp.float32
 BF16 = jnp.bfloat16
 CHUNKS = 4
+SPLIT = 124
+MOVED = 136
 
 
 def iota(shape, dim):
@@ -30,16 +32,16 @@
     return jnp.dot(a, b, preferred_element_type=F32)
 
 
-def shifted(value, first, last):
+def shifted(value, starts, ends):
     width = value.shape[1]
     lane = iota(value.shape, 1)
     zero = jnp.zeros_like(value)
     before = pltpu.roll(value, 1, 1)
     after = pltpu.roll(value, width - 1, 1)
-    if first:
-        before = jnp.where(lane == 0, zero, before)
-    if last:
-        after = jnp.where(lane == width - 1, zero, after)
+    for place in starts:
+        before = jnp.where(lane == place, zero, before)
+    for place in ends:
+        after = jnp.where(lane == place, zero, after)
     return before, after
 
 
@@ -233,10 +235,15 @@
         row_of == jnp.bitwise_and(iota(many, 0), HEIGHT - 1), dot(head_rows, tile), 0.0
     ).astype(BF16)
     first_row = HEIGHT * t
-    for b in range(BLOCKS):
-        rows = STRIDE * b - 2 + first_row + iota((24, BINS), 0)
-        gap = jnp.abs(rows - iota((24, BINS), 1)).astype(F32)
-        decay[b] = jnp.log(1.0 + gap)
+    table = (24, BINS)
+    lane = iota(table, 1)
+    for tile in range(3):
+        spot, col = STRIDE * tile, lane
+        if tile == 2:
+            spot, col = jnp.where(lane < SPLIT, 3 * STRIDE, 2 * STRIDE), jnp.where(lane < SPLIT, lane + MOVED, lane)
+        rows = spot + first_row - 2 + iota(table, 0)
+        gap = jnp.abs(rows - col).astype(F32)
+        decay[tile] = jnp.where(jnp.logical_and(rows >= 0, rows < BINS), jnp.log(1.0 + gap), 1e30)
     square = (C2, C2)
     column = jnp.sum(
         jnp.where(iota(square, 0) == iota(square, 1), jnp.broadcast_to(rate[...], square), 0.0), axis=1, keepdims=True
@@ -272,68 +279,106 @@
         stream = stream + dot(widen[l], squeezed)
     projected = dot(pair[...], jnp.maximum(stream, 0.0).astype(BF16))
     left[...] = pltpu.roll(projected[:C2], lax.rem(2 - first_row + BINS, BINS), 1)
-    right[...] = projected[C2:]
+    side = projected[C2:]
+    right[0] = side
+    right[1] = jnp.where(iota((C2, BINS), 1) < SPLIT, pltpu.roll(side, BINS - MOVED, 1), side)
+
+    narrow = iota((C2, 128), 1) < SPLIT
+    low = iota((C2, BINS), 1) < SPLIT
+
+    def put(ref, at, value, tile):
+        before, after = shifted(value, (0,) if tile == 0 else (), (BINS - 1, BINS - 1 - MOVED) if tile == 2 else (BINS - 1,))
+        lanes = pl.ds(BINS * tile, BINS)
+        ref[pl.ds(at, C2), lanes] = before
+        ref[pl.ds(at + C2, C2), lanes] = value
+        ref[pl.ds(at + 2 * C2, C2), lanes] = after
+
+    def spread_column(at):
+        return jnp.broadcast_to(left[:, at : at + 1], (C2, 128))
+
+    def pair_row(r, tile):
+        here = spread_column(STRIDE * tile + r)
+        there = jnp.where(narrow, spread_column(3 * STRIDE + r), here) if tile == 2 else here
+        decline = rates[...]
+        halves = []
+        for h, column in enumerate((there, here)):
+            lanes = slice(128 * h, 128 * h + 128)
+            fall = decline * jnp.broadcast_to(decay[tile, r : r + 1, lanes], (C2, 128))
+            halves.append(jnp.maximum(column + right[tile // 2, :, lanes] - fall, 0.0))
+        put(x1, 144 * r, jnp.concatenate(halves, axis=1).astype(BF16), tile)
+
+    def convolve(l, ref, at, rows, tile):
+        depth = 144 * (rows + 2)
+        return dot(wide_conv[l, : C2 * rows, :depth], ref[pl.ds(144 * at, depth), pl.ds(BINS * tile, BINS)])
+
+    def remix(l, convolved):
+        rows = convolved.shape[0]
+        return dot(wide_mix[l, :rows, :rows], jnp.maximum(convolved, 0.0).astype(BF16))
+
+    def first_block(at, mixed, tile):
+        for o in range(3):
+            r = at + o + 1
+            held = x1[pl.ds(144 * r + C2, C2), pl.ds(BINS * tile, BINS)].astype(F32)
+            value = held + mixed[o * C2 : (o + 1) * C2]
+            grid1[pl.ds(C2 * (r - 1), C2), pl.ds(BINS * tile, BINS)] = value
+            value = jnp.maximum(value, 0.0)
+            if tile == 0 and r == 1:
+                value = jnp.where(t == 0, 0.0, value)
+            if tile == 2 and r == HEIGHT + 2:
+                value = jnp.where(jnp.logical_and(low, t == towers - 1), 0.0, value)
+            put(x2, 144 * (r - 1), value.astype(BF16), tile)
+
+    def second_block(at, mixed, tile):
+        rows, lanes = mixed.shape[0], pl.ds(BINS * tile, BINS)
+        value = grid1[pl.ds(C2 * (at + 1), rows), lanes] + mixed
+        final[pl.ds(C2 * at, rows), lanes] = jnp.maximum(value, 0.0).astype(BF16)
+
+    groups = ((0, 3), (3, 3), (6, 3), (9, 3), (12, 2), (14, 2))
+
+    def tower(tiles):
+        for r in range(5):
+            for tile in tiles:
+                pair_row(r, tile)
+        for step in range(8):
+            ones, twos = [], []
+            if step < 6:
+                ones = [convolve(0, x1, 3 * step, 3, tile) for tile in tiles]
+            if step >= 2:
+                at, rows = groups[step - 2]
+                twos = [convolve(1, x2, at, rows, tile) for tile in tiles]
+            for r in range(3 * step + 5, min(3 * step + 8, HEIGHT + 4)):
+                for tile in tiles:
+                    pair_row(r, tile)
+            ones = [remix(0, value) for value in ones]
+            twos = [remix(1, value) for value in twos]
+            for tile, value in zip(tiles, ones):
+                first_block(3 * step, value, tile)
+            if twos:
+                for tile, value in zip(tiles, twos):
+                    second_block(at, value, tile)
 
     piece_copies = {}
-    for b in range(BLOCKS - 1, -1, -1):
-        lo = 128 if b == 3 else 0
-        width = BINS - lo
-        lanes = pl.ds(lo, width)
-        first = lo == 0
-
-        def put(ref, at, value):
-            before, after = shifted(value, first, True)
-            ref[pl.ds(at, C2), lanes] = before
-            ref[pl.ds(at + C2, C2), lanes] = value
-            ref[pl.ds(at + 2 * C2, C2), lanes] = after
-
-        base = STRIDE * b - 2 + first_row
-        decline = jnp.concatenate([rates[...]] * (width // 128), axis=1)
-        for r in range(HEIGHT + 4):
-            at = STRIDE * b + r
-            mixed = (
-                jnp.broadcast_to(left[:, at : at + 1], (C2, width))
-                + right[:, lanes]
-                - decline * jnp.broadcast_to(decay[b, r : r + 1, lanes], (C2, width))
-            )
-            mixed = jnp.maximum(mixed, 0.0)
-            if (b == 0 and r < 2) or (b == BLOCKS - 1 and r >= HEIGHT + 2):
-                mixed = jnp.where(jnp.logical_and(base + r >= 0, base + r < BINS), mixed, 0.0)
-            put(x1, 144 * r, mixed.astype(BF16))
-
-        for k in range(6):
-            convolved = dot(wide_conv[0], x1[pl.ds(432 * k, 720), lanes])
-            mixed = dot(wide_mix[0], jnp.maximum(convolved, 0.0).astype(BF16))
-            for o in range(3):
-                r = 3 * k + o + 1
-                held = x1[pl.ds(144 * r + C2, C2), lanes].astype(F32)
-                value = held + mixed[o * C2 : (o + 1) * C2]
-                grid1[pl.ds(C2 * (r - 1), C2), lanes] = value
-                value = jnp.maximum(value, 0.0)
-                if (b == 0 and r < 2) or (b == BLOCKS - 1 and r >= HEIGHT + 2):
-                    value = jnp.where(jnp.logical_and(base + r >= 0, base + r < BINS), value, 0.0)
-                put(x2, 144 * (r - 1), value.astype(BF16))
-
-        for k in range(6):
-            r0 = min(3 * k, HEIGHT - 3)
-            convolved = dot(wide_conv[1], x2[pl.ds(144 * r0, 720), lanes])
-            mixed = dot(wide_mix[1], jnp.maximum(convolved, 0.0).astype(BF16))
-            value = grid1[pl.ds(C2 * (r0 + 1), 144), lanes] + mixed
-            final[pl.ds(C2 * r0, 144), lanes] = jnp.maximum(value, 0.0).astype(BF16)
-
-        contact = dot(wide_head[...], final[:, lanes])
-        if lo:
-            contact = jnp.concatenate([jnp.zeros((TARGETS * HEIGHT, lo), F32), contact], axis=1)
-        contact = contact.reshape(TARGETS, HEIGHT, BINS)
-        turn = lax.rem(2 * BINS - STRIDE * b - first_row, BINS)
-        piece = skewed(pltpu.roll(contact, turn, 2), -1) * row_weights[b][None]
-        if b == 0:
-            own_piece[...] = piece
-        else:
-            span = BINS if b == 1 else 128
-            sent[b - 1] = piece.astype(BF16)
-            source, target = (ref.at[b - 1, :, :, pl.ds(0, span)] for ref in (sent, landed))
-            piece_copies[b] = send(source, target, piece_send.at[b - 1], piece_recv.at[b - 1], at_genome(b))
+
+    def piece_of(b, contact):
+        start = STRIDE * b + first_row - (MOVED if b == 3 else 0)
+        return skewed(pltpu.roll(contact, lax.rem(2 * BINS - start, BINS), 2), -1) * row_weights[b][None]
+
+    def hand_on(b, piece):
+        span = BINS if b == 1 else 128
+        sent[b - 1] = piece.astype(BF16)
+        source, target = (ref.at[b - 1, :, :, pl.ds(0, span)] for ref in (sent, landed))
+        piece_copies[b] = send(source, target, piece_send.at[b - 1], piece_recv.at[b - 1], at_genome(b))
+
+    def contact_of(tile):
+        return dot(wide_head[...], final[:, pl.ds(BINS * tile, BINS)]).reshape(TARGETS, HEIGHT, BINS)
+
+    tower((1, 2))
+    contact = contact_of(2)
+    hand_on(3, piece_of(3, contact))
+    hand_on(2, piece_of(2, contact))
+    hand_on(1, piece_of(1, contact_of(1)))
+    tower((0,))
+    own_piece[...] = piece_of(0, contact_of(0))
 
     for b, copy in piece_copies.items():
         receive(copy, g >= b)
@@ -423,15 +468,15 @@
                 vmem((2, 3 * C2, 15 * C2), BF16),
                 vmem((2, 3 * C2, 3 * C2), BF16),
                 vmem((many, HEIGHT * C2), BF16),
-                vmem((BLOCKS, 24, BINS), F32),
+                vmem((3, 24, BINS), F32),
                 vmem((C2, 128), F32),
                 vmem((BLOCKS + 1, HEIGHT, BINS), F32),
                 vmem((C2, BINS), F32),
-                vmem((C2, BINS), F32),
-                vmem((20 * 144, BINS), BF16),
-                vmem((18 * 144, BINS), BF16),
-                vmem((18 * C2, BINS), F32),
-                vmem((HEIGHT * C2, BINS), BF16),
+                vmem((2, C2, BINS), F32),
+                vmem((20 * 144, 3 * BINS), BF16),
+                vmem((18 * 144, 3 * BINS), BF16),
+                vmem((18 * C2, 3 * BINS), F32),
+                vmem((HEIGHT * C2, 3 * BINS), BF16),
                 vmem((BLOCKS - 1, TARGETS, HEIGHT, BINS), BF16),
                 vmem((BLOCKS - 1, TARGETS, HEIGHT, BINS), BF16),
                 vmem((TARGETS, HEIGHT, BINS), F32),

time: 37.4 us -> 29.4 us (0.79)
  the two profiles are of different devices: /device:TPU:256 before, /device:TPU:257 now
where the time goes in v3:
time: 29.4 us; the launch traced here: 29.2 us
  Pallas kernels  28.5 us (97%)
  between operations  0.64 us (2%)
    pallas_call x1, Pallas kernels, per_device(): pl.pallas_call(functools.partial(kernel, genomes, towers), out_shape=shap...  27 us
    pallas_call x1, Pallas kernels, per_device(): pl.pallas_call(hand_over, out_shape=shapes, in_specs=[in_vmem, in_vmem],...  1.54 us

profile of v3, /device:TPU:257, one launch (start us, length us, event | category | flops | bytes accessed | tf_op | source)
XLA Modules:
  0.0 29.2 jit_solution(10779839902602655072)
XLA Ops:
  0.6 27.0 %contacts.1 = (f32[5,16,256]{2,1,0:T(8,128)}, f32[5,2,16]{2,1,0:T(2,128)}) custom-call(s32[1024,128]{1,0:T(8,128)} %bitcast.5, s32[1,256]{1,0:T(1,128)} %bitcast.7, bf16[96,8192]{1,0:T(8,128)(2,1)} %stem_hbm.1, bf16[6,48,288]{2,1,0:T(8,128)(2,1)} %trunk_in_hbm.1, bf16[6,48,96]{2,1,0:T(8,128)(2,1)} %bitcast.6, bf16[96,96]{1,0:T(8,128)(2,1)} %pair_hbm.1, ...), custom_call_target="tpu_custom_call" | custom-call | tf_op jit(solution)/shard_map/contacts/pallas_call | solution.py:448
  27.6 1.5 %hand_over.1 = (f32[5,16,256]{2,1,0:T(8,128)}, f32[5,2,16]{2,1,0:T(2,128)}) custom-call(f32[5,16,256]{2,1,0:T(8,128)} %get-tuple-element.6.band, f32[5,2,16]{2,1,0:T(2,128)} %get-tuple-element.7.scores), custom_call_target="tpu_custom_call" | custom-call | tf_op jit(solution)/shard_map/hand_over/pallas_call | solution.py:508

commit v4 on v3

--- a/solution.py
+++ b/solution.py
@@ -19,7 +19,7 @@
 HEIGHT = 16
 F32 = jnp.float32
 BF16 = jnp.bfloat16
-CHUNKS = 4
+CHUNKS = 2
 SPLIT = 124
 MOVED = 136
 
@@ -43,15 +43,6 @@
     for place in ends:
         after = jnp.where(lane == place, zero, after)
     return before, after
-
-
-def skewed(value, sign):
-    width = value.shape[2]
-    row = iota(value.shape, 1)
-    for bit in (1, 2, 4, 8):
-        turned = pltpu.roll(value, bit if sign > 0 else width - bit, 2)
-        value = jnp.where(jnp.bitwise_and(row, bit) != 0, turned, value)
-    return value
 
 
 def kernel(
@@ -79,7 +70,6 @@
     conv,
     mix,
     head,
-    onehot,
     window,
     taps,
     widen,
@@ -88,6 +78,7 @@
     wide_head,
     decay,
     rates,
+    runs,
     row_weights,
     left,
     right,
@@ -122,16 +113,6 @@
         near = {"genome": g + up, "tower": t + step - up * towers}
         return near, jnp.logical_and(place + step >= 0, place + step < genomes * towers)
 
-    barrier = pltpu.get_barrier_semaphore()
-    steps = (-1, 1, -2, 2, -3, 3)
-    present = jnp.int32(0)
-    for device, there in [at_genome(s) for s in steps] + [at_band(s) for s in steps]:
-        present = present + there.astype(jnp.int32)
-
-        @pl.when(there)
-        def _():
-            pl.semaphore_signal(barrier, inc=1, device_id=device, device_id_type=pl.DeviceIdType.MESH)
-
     chunk = 4 * BP // CHUNKS
     bases_copy = pltpu.make_async_copy(bases_hbm, bases, in_sems.at[0])
     bases_copy.start()
@@ -154,19 +135,39 @@
     for copy in small_copies:
         copy.start()
 
+    barrier = pltpu.get_barrier_semaphore()
+    steps = (-1, 1, -2, 2, -3, 3)
+    present = jnp.int32(0)
+    for device, there in [at_genome(s) for s in steps] + [at_band(s) for s in steps]:
+        present = present + there.astype(jnp.int32)
+
+        @pl.when(there)
+        def _():
+            pl.semaphore_signal(barrier, inc=1, device_id=device, device_id_type=pl.DeviceIdType.MESH)
+
     bases_copy.wait()
-    spread = jnp.where(lax.shift_right_logical(iota((128, 512), 1), 2) == iota((128, 512), 0), 1.0, 0.0).astype(BF16)
-    letter = jnp.bitwise_and(iota((STRIDE, 512), 1), 3).astype(F32)
-    summed = jnp.zeros((STRIDE, C1), F32)
-    for k in range(CHUNKS):
-        for q in range(16 // CHUNKS):
-            rows = bases[pl.ds(k * (16 // CHUNKS) + q, STRIDE, stride=16), :]
-            repeated = dot(rows.astype(F32).astype(BF16), spread)
-            onehot[:, pl.ds(q * 512, 512)] = jnp.where(repeated == letter, 1.0, 0.0).astype(BF16)
-        stem_copies[k].wait()
-        summed = summed + lax.dot_general(
-            onehot[...], stem[:, pl.ds(k * chunk, chunk)], (((1,), (1,)), ((), ())), preferred_element_type=F32
+    code = bases[pl.ds(0, STRIDE, stride=16), :]
+    for k in range(1, 16):
+        code = jnp.bitwise_or(code, lax.shift_left(bases[pl.ds(k, STRIDE, stride=16), :], jnp.int32(2 * k)))
+    for copy in stem_copies:
+        copy.wait()
+    lane = iota((STRIDE, 128), 1)
+    spread = [jnp.take_along_axis(code, lax.shift_right_logical(lane, 2) + 32 * m, axis=1) for m in range(4)]
+    letter = jnp.bitwise_and(lane, 3)
+    sums = []
+    for k in range(16):
+        mask = (3 << 2 * k) - (1 << 32 if k == 15 else 0)
+        wanted = lax.shift_left(letter, jnp.int32(2 * k))
+        hits = [jnp.where(jnp.bitwise_and(value, jnp.int32(mask)) == wanted, 1.0, 0.0) for value in spread]
+        sums.append(
+            lax.dot_general(
+                jnp.concatenate(hits, axis=1).astype(BF16),
+                stem[:, pl.ds(512 * k, 512)],
+                (((1,), (1,)), ((), ())),
+                preferred_element_type=F32,
+            )
         )
+    summed = sum(sums[1:], sums[0])
     window[0] = jnp.concatenate([summed, jnp.zeros((STRIDE, 128 - C1), F32)], axis=1).astype(BF16)
 
     pl.semaphore_wait(barrier, present)
@@ -226,13 +227,12 @@
     lane = iota((C2, HEIGHT * C2), 1)
     row_of = lax.shift_right_logical(lane * 1366, 16)
     tile = jnp.where(lane - row_of * C2 == iota((C2, HEIGHT * C2), 0), 1.0, 0.0).astype(BF16)
-    head_rows = jnp.concatenate(
-        [jnp.broadcast_to(head[k : k + 1].astype(F32), (HEIGHT, C2)) for k in range(TARGETS)], axis=0
-    ).astype(BF16)
-    many = (TARGETS * HEIGHT, HEIGHT * C2)
+    padded = jnp.concatenate([head[...].astype(F32), jnp.zeros((8 - TARGETS, C2), F32)], axis=0)
+    head_rows = jnp.concatenate([padded] * HEIGHT, axis=0).astype(BF16)
+    many = (8 * HEIGHT, HEIGHT * C2)
     row_of = lax.shift_right_logical(iota(many, 1) * 1366, 16)
     wide_head[...] = jnp.where(
-        row_of == jnp.bitwise_and(iota(many, 0), HEIGHT - 1), dot(head_rows, tile), 0.0
+        row_of == lax.shift_right_logical(iota(many, 0), 3), dot(head_rows, tile), 0.0
     ).astype(BF16)
     first_row = HEIGHT * t
     table = (24, BINS)
@@ -244,6 +244,10 @@
         rows = spot + first_row - 2 + iota(table, 0)
         gap = jnp.abs(rows - col).astype(F32)
         decay[tile] = jnp.where(jnp.logical_and(rows >= 0, rows < BINS), jnp.log(1.0 + gap), 1e30)
+    span = (2 * 128, 128)
+    ahead = jnp.bitwise_and(iota(span, 0), 127) - iota(span, 1)
+    taken = jnp.logical_and(jnp.logical_and(ahead >= 1, ahead <= STRIDE), iota(span, 1) < STRIDE)
+    runs[...] = jnp.where(taken, 1.0, 0.0).astype(BF16)
     square = (C2, C2)
     column = jnp.sum(
         jnp.where(iota(square, 0) == iota(square, 1), jnp.broadcast_to(rate[...], square), 0.0), axis=1, keepdims=True
@@ -335,88 +339,87 @@
 
     groups = ((0, 3), (3, 3), (6, 3), (9, 3), (12, 2), (14, 2))
 
-    def tower(tiles):
-        for r in range(5):
-            for tile in tiles:
+    def tower(work):
+        ones = [(tile, step, convolve(0, x1, 3 * step, 3, tile)) for tile, step in work if 0 <= step < 6]
+        twos = [(tile, groups[step - 2], convolve(1, x2, *groups[step - 2], tile)) for tile, step in work if 2 <= step < 8]
+        for tile, step in work:
+            for r in range(3 * step + 5 if step >= 0 else 0, min(3 * step + 8, HEIGHT + 4) if step >= -1 else 0):
                 pair_row(r, tile)
-        for step in range(8):
-            ones, twos = [], []
-            if step < 6:
-                ones = [convolve(0, x1, 3 * step, 3, tile) for tile in tiles]
-            if step >= 2:
-                at, rows = groups[step - 2]
-                twos = [convolve(1, x2, at, rows, tile) for tile in tiles]
-            for r in range(3 * step + 5, min(3 * step + 8, HEIGHT + 4)):
-                for tile in tiles:
-                    pair_row(r, tile)
-            ones = [remix(0, value) for value in ones]
-            twos = [remix(1, value) for value in twos]
-            for tile, value in zip(tiles, ones):
-                first_block(3 * step, value, tile)
-            if twos:
-                for tile, value in zip(tiles, twos):
-                    second_block(at, value, tile)
+        ones = [(tile, step, remix(0, value)) for tile, step, value in ones]
+        twos = [(tile, group, remix(1, value)) for tile, group, value in twos]
+        for tile, step, value in ones:
+            first_block(3 * step, value, tile)
+        for tile, group, value in twos:
+            second_block(group[0], value, tile)
 
     piece_copies = {}
 
     def piece_of(b, contact):
         start = STRIDE * b + first_row - (MOVED if b == 3 else 0)
-        return skewed(pltpu.roll(contact, lax.rem(2 * BINS - start, BINS), 2), -1) * row_weights[b][None]
+        span = BINS if b < 2 else 128
+        rows = []
+        for r in range(HEIGHT):
+            turned = pltpu.roll(contact[8 * r : 8 * r + 8], lax.rem(2 * BINS - r - start, BINS), 1)
+            rows.append(turned[:, :span] * row_weights[b, r : r + 1, :span])
+        return jnp.concatenate(rows, axis=0)
 
     def hand_on(b, piece):
-        span = BINS if b == 1 else 128
-        sent[b - 1] = piece.astype(BF16)
-        source, target = (ref.at[b - 1, :, :, pl.ds(0, span)] for ref in (sent, landed))
+        span = piece.shape[1]
+        sent[b - 1, :, :span] = piece.astype(BF16)
+        source, target = (ref.at[b - 1, :, pl.ds(0, span)] for ref in (sent, landed))
         piece_copies[b] = send(source, target, piece_send.at[b - 1], piece_recv.at[b - 1], at_genome(b))
 
     def contact_of(tile):
-        return dot(wide_head[...], final[:, pl.ds(BINS * tile, BINS)]).reshape(TARGETS, HEIGHT, BINS)
-
-    tower((1, 2))
-    contact = contact_of(2)
-    hand_on(3, piece_of(3, contact))
-    hand_on(2, piece_of(2, contact))
-    hand_on(1, piece_of(1, contact_of(1)))
-    tower((0,))
+        return dot(wide_head[...], final[:, pl.ds(BINS * tile, BINS)])
+
+    lags = (6,3,0)
+    for moment in range(-1, lags[0] + 9):
+        tower([(tile, moment - lags[tile]) for tile in (2, 1, 0)])
+        if moment == lags[2] + 8:
+            contact = contact_of(2)
+            hand_on(3, piece_of(3, contact))
+            hand_on(2, piece_of(2, contact))
+        if moment == lags[1] + 8:
+            hand_on(1, piece_of(1, contact_of(1)))
     own_piece[...] = piece_of(0, contact_of(0))
 
     for b, copy in piece_copies.items():
         receive(copy, g >= b)
-    near = own_piece[:, :, :128]
+    near = own_piece[:, :128]
     for b in range(1, BLOCKS):
-        near = near + jnp.where(g >= b, landed[b - 1, :, :, :128].astype(F32), 0.0)
-    far = own_piece[:, :, 128:] + jnp.where(g >= 1, landed[0, :, :, 128:].astype(F32), 0.0)
-    near = near * row_weights[BLOCKS, :, :128][None]
-    band[:, :, :128] = near
-    band[:, :, 128:] = far * row_weights[BLOCKS, :, 128:][None]
-
-    shape = (TARGETS, HEIGHT, 128)
-    lane = iota(shape, 2)
-    run = near
-    for step in (1, 2, 4, 8, 16, 32):
-        run = run + pltpu.roll(run, 128 - step, 2)
-    inside = jnp.where(jnp.logical_and(lane >= 1, lane <= STRIDE), run, 0.0)
-    insulation = jnp.sum(skewed(pltpu.roll(inside, 127, 2), 1), axis=1)
-    contact = jnp.where(jnp.logical_and(lane >= 1, lane <= STRIDE), jnp.exp(near), 0.0)
-    upstream = jnp.sum(skewed(contact, 1), axis=1)
-    downstream = jnp.sum(contact, axis=2, keepdims=True)
-    downstream = jnp.sum(jnp.where(lane == iota(shape, 1), jnp.broadcast_to(downstream, shape), 0.0), axis=1)
-    part[0:TARGETS] = insulation
-    part[8 : 8 + TARGETS] = upstream
+        near = near + jnp.where(g >= b, landed[b - 1, :, :128].astype(F32), 0.0)
+    far = own_piece[:, 128:] + jnp.where(g >= 1, landed[0, :, 128:].astype(F32), 0.0)
+    near = [near[8 * r : 8 * r + 8] * row_weights[BLOCKS, r : r + 1, :128] for r in range(HEIGHT)]
+
+    lane = iota((8, 128), 1)
+    counted = jnp.logical_and(lane >= 1, lane <= STRIDE)
+    joined = jnp.concatenate(near, axis=0)
+    coarse = joined.astype(BF16)
+    fine = (joined - coarse.astype(F32)).astype(BF16)
+    squares = dot(jnp.concatenate([coarse, fine], axis=1), runs[...])
+    insulation = upstream = downstream = jnp.zeros((8, 128), F32)
+    for r in range(HEIGHT):
+        insulation = insulation + pltpu.roll(squares[8 * r : 8 * r + 8], r, 1)
+        contact = jnp.where(counted, jnp.exp(near[r]), 0.0)
+        upstream = upstream + pltpu.roll(contact, r, 1)
+        downstream = jnp.where(lane == r, jnp.sum(contact, axis=1, keepdims=True), downstream)
+    part[0:8] = insulation
+    part[8:16] = upstream
     part_copies = [
         send(part, parts_in.at[m - 1], part_send.at[m - 1], part_recv.at[m - 1], at_band(m)) for m in range(1, BLOCKS + 1)
     ]
+    for r in range(HEIGHT):
+        band[:, r, :128] = near[r][:TARGETS]
+        band[:, r, 128:] = (far[8 * r : 8 * r + 8] * row_weights[BLOCKS, r : r + 1, 128:])[:TARGETS]
     for m, copy in enumerate(part_copies):
         receive(copy, place > m)
-    flat = (TARGETS, 128)
-    lane = iota(flat, 1)
     for m in range(1, BLOCKS + 1):
         turn = 128 - HEIGHT * m
         absent = float(HEIGHT) if m < BLOCKS else (HEIGHT - lane).astype(F32)
-        insulation = insulation + jnp.where(place >= m, pltpu.roll(parts_in[m - 1, 0:TARGETS], turn, 1), 0.0)
-        upstream = upstream + jnp.where(place >= m, pltpu.roll(parts_in[m - 1, 8 : 8 + TARGETS], turn, 1), absent)
-    scores[:, 0, :] = (insulation * (1.0 / (STRIDE * STRIDE)))[:, :HEIGHT]
-    scores[:, 1, :] = ((downstream - upstream) / (downstream + upstream))[:, :HEIGHT]
+        insulation = insulation + jnp.where(place >= m, pltpu.roll(parts_in[m - 1, 0:8], turn, 1), 0.0)
+        upstream = upstream + jnp.where(place >= m, pltpu.roll(parts_in[m - 1, 8:16], turn, 1), absent)
+    scores[:, 0, :] = (insulation * (1.0 / (STRIDE * STRIDE)))[:TARGETS, :HEIGHT]
+    scores[:, 1, :] = ((downstream - upstream) / (downstream + upstream))[:TARGETS, :HEIGHT]
     for copy, there in sends:
 
         @pl.when(there)
@@ -439,7 +442,7 @@
         anywhere = pl.BlockSpec(memory_space=pl.ANY)
         vmem = pltpu.VMEM
         dma = pltpu.SemaphoreType.DMA
-        many = TARGETS * HEIGHT
+        many = 8 * HEIGHT
         shapes = (
             jax.ShapeDtypeStruct((TARGETS, HEIGHT, BINS), F32),
             jax.ShapeDtypeStruct((TARGETS, 2, HEIGHT), F32),
@@ -461,7 +464,6 @@
                 vmem((2, 3, C2, 3 * C2), BF16),
                 vmem((2, C2, C2), BF16),
                 vmem((TARGETS, C2), BF16),
-                vmem((STRIDE, 4 * BP // CHUNKS), BF16),
                 vmem((BLOCKS, STRIDE, 128), BF16),
                 vmem((TRUNK, 3 * MID, C1), BF16),
                 vmem((TRUNK, C1, MID), BF16),
@@ -470,6 +472,7 @@
                 vmem((many, HEIGHT * C2), BF16),
                 vmem((3, 24, BINS), F32),
                 vmem((C2, 128), F32),
+                vmem((2 * 128, 128), BF16),
                 vmem((BLOCKS + 1, HEIGHT, BINS), F32),
                 vmem((C2, BINS), F32),
                 vmem((2, C2, BINS), F32),
@@ -477,9 +480,9 @@
                 vmem((18 * 144, 3 * BINS), BF16),
                 vmem((18 * C2, 3 * BINS), F32),
                 vmem((HEIGHT * C2, 3 * BINS), BF16),
-                vmem((BLOCKS - 1, TARGETS, HEIGHT, BINS), BF16),
-                vmem((BLOCKS - 1, TARGETS, HEIGHT, BINS), BF16),
-                vmem((TARGETS, HEIGHT, BINS), F32),
+                vmem((BLOCKS - 1, many, BINS), BF16),
+                vmem((BLOCKS - 1, many, BINS), BF16),
+                vmem((many, BINS), F32),
                 vmem((16, 128), F32),
                 vmem((BLOCKS, 16, 128), F32),
                 dma((9,)),

time: 29.4 us -> 29.4 us (level)
  no operation moved by 1% of the time
where the time goes in v4:
time: 29.4 us; the launch traced here: 29.2 us
  Pallas kernels  28.6 us (97%)
  between operations  0.64 us (2%)
    pallas_call x1, Pallas kernels, per_device(): pl.pallas_call(functools.partial(kernel, genomes, towers), out_shape=shap...  27 us
    pallas_call x1, Pallas kernels, per_device(): pl.pallas_call(hand_over, out_shape=shapes, in_specs=[in_vmem, in_vmem],...  1.54 us

profile of v4, /device:TPU:257, one launch (start us, length us, event | category | flops | bytes accessed | tf_op | source)
XLA Modules:
  0.0 29.2 jit_solution(725293531897196420)
XLA Ops:
  0.6 27.0 %contacts.1 = (f32[5,16,256]{2,1,0:T(8,128)}, f32[5,2,16]{2,1,0:T(2,128)}) custom-call(s32[1024,128]{1,0:T(8,128)} %bitcast.5, s32[1,256]{1,0:T(1,128)} %bitcast.7, bf16[96,8192]{1,0:T(8,128)(2,1)} %stem_hbm.1, bf16[6,48,288]{2,1,0:T(8,128)(2,1)} %trunk_in_hbm.1, bf16[6,48,96]{2,1,0:T(8,128)(2,1)} %bitcast.6, bf16[96,96]{1,0:T(8,128)(2,1)} %pair_hbm.1, ...), custom_call_target="tpu_custom_call" | custom-call | tf_op jit(solution)/shard_map/contacts/pallas_call | solution.py:451
  27.7 1.5 %hand_over.1 = (f32[5,16,256]{2,1,0:T(8,128)}, f32[5,2,16]{2,1,0:T(2,128)}) custom-call(f32[5,16,256]{2,1,0:T(8,128)} %get-tuple-element.6.band, f32[5,2,16]{2,1,0:T(2,128)} %get-tuple-element.7.scores), custom_call_target="tpu_custom_call" | custom-call | tf_op jit(solution)/shard_map/hand_over/pallas_call | solution.py:511

commit v5 on v4

--- a/solution.py
+++ b/solution.py
@@ -136,14 +136,22 @@
         copy.start()
 
     barrier = pltpu.get_barrier_semaphore()
-    steps = (-1, 1, -2, 2, -3, 3)
-    present = jnp.int32(0)
-    for device, there in [at_genome(s) for s in steps] + [at_band(s) for s in steps]:
-        present = present + there.astype(jnp.int32)
+    met = jnp.int32(towers - 1)
+    for s in range(1, BLOCKS):
+        met = met + (g >= s).astype(jnp.int32)
+        device, there = at_genome(s)
 
         @pl.when(there)
         def _():
             pl.semaphore_signal(barrier, inc=1, device_id=device, device_id_type=pl.DeviceIdType.MESH)
+
+    for s in range(1, towers):
+        pl.semaphore_signal(
+            barrier,
+            inc=1,
+            device_id={"genome": g, "tower": lax.rem(t + s, towers)},
+            device_id_type=pl.DeviceIdType.MESH,
+        )
 
     bases_copy.wait()
     code = bases[pl.ds(0, STRIDE, stride=16), :]
@@ -170,7 +178,7 @@
     summed = sum(sums[1:], sums[0])
     window[0] = jnp.concatenate([summed, jnp.zeros((STRIDE, 128 - C1), F32)], axis=1).astype(BF16)
 
-    pl.semaphore_wait(barrier, present)
+    pl.semaphore_wait(barrier, met)
     sends = []
 
     def send(source, target, send_sem, recv_sem, to):
@@ -372,7 +380,7 @@
     def contact_of(tile):
         return dot(wide_head[...], final[:, pl.ds(BINS * tile, BINS)])
 
-    lags = (6,3,0)
+    lags = (6,0,0)
     for moment in range(-1, lags[0] + 9):
         tower([(tile, moment - lags[tile]) for tile in (2, 1, 0)])
         if moment == lags[2] + 8:

time: 29.4 us -> 29.5 us (level)
  no operation moved by 1% of the time
where the time goes in v5:
time: 29.5 us; the launch traced here: 29.3 us
  Pallas kernels  28.6 us (97%)
  between operations  0.64 us (2%)
    pallas_call x1, Pallas kernels, per_device(): pl.pallas_call(functools.partial(kernel, genomes, towers), out_shape=shap...  27.1 us
    pallas_call x1, Pallas kernels, per_device(): pl.pallas_call(hand_over, out_shape=shapes, in_specs=[in_vmem, in_vmem],...  1.54 us

profile of v5, /device:TPU:257, one launch (start us, length us, event | category | flops | bytes accessed | tf_op | source)
XLA Modules:
  0.0 29.3 jit_solution(1273273218311958064)
XLA Ops:
  0.6 27.1 %contacts.1 = (f32[5,16,256]{2,1,0:T(8,128)}, f32[5,2,16]{2,1,0:T(2,128)}) custom-call(s32[1024,128]{1,0:T(8,128)} %bitcast.5, s32[1,256]{1,0:T(1,128)} %bitcast.7, bf16[96,8192]{1,0:T(8,128)(2,1)} %stem_hbm.1, bf16[6,48,288]{2,1,0:T(8,128)(2,1)} %trunk_in_hbm.1, bf16[6,48,96]{2,1,0:T(8,128)(2,1)} %bitcast.6, bf16[96,96]{1,0:T(8,128)(2,1)} %pair_hbm.1, ...), custom_call_target="tpu_custom_call" | custom-call | tf_op jit(solution)/shard_map/contacts/pallas_call | solution.py:459
  27.7 1.5 %hand_over.1 = (f32[5,16,256]{2,1,0:T(8,128)}, f32[5,2,16]{2,1,0:T(2,128)}) custom-call(f32[5,16,256]{2,1,0:T(8,128)} %get-tuple-element.6.band, f32[5,2,16]{2,1,0:T(2,128)} %get-tuple-element.7.scores), custom_call_target="tpu_custom_call" | custom-call | tf_op jit(solution)/shard_map/hand_over/pallas_call | solution.py:519

commit v6 on v5

--- a/solution.py
+++ b/solution.py
@@ -88,6 +88,8 @@
     final,
     sent,
     landed,
+    squeeze,
+    expand,
     own_piece,
     part,
     parts_in,
@@ -242,6 +244,15 @@
     wide_head[...] = jnp.where(
         row_of == lax.shift_right_logical(iota(many, 0), 3), dot(head_rows, tile), 0.0
     ).astype(BF16)
+    small = (TARGETS * HEIGHT, 8 * HEIGHT)
+    row_of = lax.shift_right_logical(iota(small, 0) * 205, 10)
+    squeeze[...] = jnp.where(iota(small, 1) == iota(small, 0) + 3 * row_of, 1.0, 0.0).astype(BF16)
+    large = (8 * HEIGHT, 3 * TARGETS * HEIGHT)
+    row, lane = iota(large, 0), iota(large, 1)
+    lane = lane - TARGETS * HEIGHT * ((lane >= TARGETS * HEIGHT).astype(jnp.int32) + (lane >= 2 * TARGETS * HEIGHT).astype(jnp.int32))
+    target = jnp.bitwise_and(row, 7)
+    at = TARGETS * lax.shift_right_logical(row, 3) + target
+    expand[...] = jnp.where(jnp.logical_and(target < TARGETS, lane == at), 1.0, 0.0).astype(BF16)
     first_row = HEIGHT * t
     table = (24, BINS)
     lane = iota(table, 1)
@@ -373,30 +384,32 @@
 
     def hand_on(b, piece):
         span = piece.shape[1]
-        sent[b - 1, :, :span] = piece.astype(BF16)
-        source, target = (ref.at[b - 1, :, pl.ds(0, span)] for ref in (sent, landed))
+        sent[b - 1, :, :span] = dot(squeeze[...], piece.astype(BF16)).astype(BF16)
+        source = sent.at[b - 1, :, pl.ds(0, span)]
+        target = landed.at[pl.ds(TARGETS * HEIGHT * (b - 1), TARGETS * HEIGHT), pl.ds(0, span)]
         piece_copies[b] = send(source, target, piece_send.at[b - 1], piece_recv.at[b - 1], at_genome(b))
 
     def contact_of(tile):
         return dot(wide_head[...], final[:, pl.ds(BINS * tile, BINS)])
 
-    lags = (6,0,0)
+    lags = (9,0,0)
     for moment in range(-1, lags[0] + 9):
         tower([(tile, moment - lags[tile]) for tile in (2, 1, 0)])
-        if moment == lags[2] + 8:
+        if moment == lags[1] + 8:
+            hand_on(1, piece_of(1, contact_of(1)))
             contact = contact_of(2)
             hand_on(3, piece_of(3, contact))
             hand_on(2, piece_of(2, contact))
-        if moment == lags[1] + 8:
-            hand_on(1, piece_of(1, contact_of(1)))
     own_piece[...] = piece_of(0, contact_of(0))
 
     for b, copy in piece_copies.items():
         receive(copy, g >= b)
-    near = own_piece[:, :128]
-    for b in range(1, BLOCKS):
-        near = near + jnp.where(g >= b, landed[b - 1, :, :128].astype(F32), 0.0)
-    far = own_piece[:, 128:] + jnp.where(g >= 1, landed[0, :, 128:].astype(F32), 0.0)
+    rows = TARGETS * HEIGHT
+    arrived = jnp.concatenate(
+        [jnp.where(g >= b, landed[rows * (b - 1) : rows * b, :128].astype(F32), 0.0) for b in range(1, BLOCKS)], axis=0
+    )
+    near = own_piece[:, :128] + dot(expand[...], arrived.astype(BF16))
+    arrived = jnp.where(g >= 1, landed[:rows, 128:].astype(F32), 0.0)
     near = [near[8 * r : 8 * r + 8] * row_weights[BLOCKS, r : r + 1, :128] for r in range(HEIGHT)]
 
     lane = iota((8, 128), 1)
@@ -416,6 +429,7 @@
     part_copies = [
         send(part, parts_in.at[m - 1], part_send.at[m - 1], part_recv.at[m - 1], at_band(m)) for m in range(1, BLOCKS + 1)
     ]
+    far = own_piece[:, 128:] + dot(expand[:, :rows], arrived.astype(BF16))
     for r in range(HEIGHT):
         band[:, r, :128] = near[r][:TARGETS]
         band[:, r, 128:] = (far[8 * r : 8 * r + 8] * row_weights[BLOCKS, r : r + 1, 128:])[:TARGETS]
@@ -488,8 +502,10 @@
                 vmem((18 * 144, 3 * BINS), BF16),
                 vmem((18 * C2, 3 * BINS), F32),
                 vmem((HEIGHT * C2, 3 * BINS), BF16),
-                vmem((BLOCKS - 1, many, BINS), BF16),
-                vmem((BLOCKS - 1, many, BINS), BF16),
+                vmem((BLOCKS - 1, TARGETS * HEIGHT, BINS), BF16),
+                vmem(((BLOCKS - 1) * TARGETS * HEIGHT, BINS), BF16),
+                vmem((TARGETS * HEIGHT, many), BF16),
+                vmem((many, 3 * TARGETS * HEIGHT), BF16),
                 vmem((many, BINS), F32),
                 vmem((16, 128), F32),
                 vmem((BLOCKS, 16, 128), F32),

time: 29.5 us -> 28.5 us (0.966)
  Pallas kernels: 28.6 us -> 27.6 us
    pallas_call x1, Pallas kernels: 27.1 us -> 26.1 us  [per_device(): pl.pallas_call(functools.partial(kernel, genomes, towers), out_shape=shap...]
where the time goes in v6:
time: 28.5 us; the launch traced here: 28.3 us
  Pallas kernels  27.6 us (97%)
  between operations  0.64 us (2%)
    pallas_call x1, Pallas kernels, per_device(): pl.pallas_call(functools.partial(kernel, genomes, towers), out_shape=shap...  26.1 us
    pallas_call x1, Pallas kernels, per_device(): pl.pallas_call(hand_over, out_shape=shapes, in_specs=[in_vmem, in_vmem],...  1.54 us

profile of v6, /device:TPU:257, one launch (start us, length us, event | category | flops | bytes accessed | tf_op | source)
XLA Modules:
  0.0 28.3 jit_solution(12224629834655832477)
XLA Ops:
  0.6 26.1 %contacts.1 = (f32[5,16,256]{2,1,0:T(8,128)}, f32[5,2,16]{2,1,0:T(2,128)}) custom-call(s32[1024,128]{1,0:T(8,128)} %bitcast.5, s32[1,256]{1,0:T(1,128)} %bitcast.7, bf16[96,8192]{1,0:T(8,128)(2,1)} %stem_hbm.1, bf16[6,48,288]{2,1,0:T(8,128)(2,1)} %trunk_in_hbm.1, bf16[6,48,96]{2,1,0:T(8,128)(2,1)} %bitcast.6, bf16[96,96]{1,0:T(8,128)(2,1)} %pair_hbm.1, ...), custom_call_target="tpu_custom_call" | custom-call | tf_op jit(solution)/shard_map/contacts/pallas_call | solution.py:473
  26.7 1.5 %hand_over.1 = (f32[5,16,256]{2,1,0:T(8,128)}, f32[5,2,16]{2,1,0:T(2,128)}) custom-call(f32[5,16,256]{2,1,0:T(8,128)} %get-tuple-element.6.band, f32[5,2,16]{2,1,0:T(2,128)} %get-tuple-element.7.scores), custom_call_target="tpu_custom_call" | custom-call | tf_op jit(solution)/shard_map/hand_over/pallas_call | solution.py:535

commit v7 on v6

--- a/solution.py
+++ b/solution.py
@@ -427,14 +427,14 @@
     part[0:8] = insulation
     part[8:16] = upstream
     part_copies = [
-        send(part, parts_in.at[m - 1], part_send.at[m - 1], part_recv.at[m - 1], at_band(m)) for m in range(1, BLOCKS + 1)
+        send(part, parts_in.at[m - 1], part_send.at[m - 1], part_recv.at[m - 1], at_band(m)) for m in (3, 2, 4, 1)
     ]
     far = own_piece[:, 128:] + dot(expand[:, :rows], arrived.astype(BF16))
     for r in range(HEIGHT):
         band[:, r, :128] = near[r][:TARGETS]
         band[:, r, 128:] = (far[8 * r : 8 * r + 8] * row_weights[BLOCKS, r : r + 1, 128:])[:TARGETS]
-    for m, copy in enumerate(part_copies):
-        receive(copy, place > m)
+    for m, copy in zip((3, 2, 4, 1), part_copies):
+        receive(copy, place >= m)
     for m in range(1, BLOCKS + 1):
         turn = 128 - HEIGHT * m
         absent = float(HEIGHT) if m < BLOCKS else (HEIGHT - lane).astype(F32)

time: 28.5 us -> 28.5 us (level)
  no operation moved by 1% of the time
where the time goes in v7:
time: 28.5 us; the launch traced here: 28.3 us
  Pallas kernels  27.7 us (97%)
  between operations  0.64 us (2%)
    pallas_call x1, Pallas kernels, per_device(): pl.pallas_call(functools.partial(kernel, genomes, towers), out_shape=shap...  26.1 us
    pallas_call x1, Pallas kernels, per_device(): pl.pallas_call(hand_over, out_shape=shapes, in_specs=[in_vmem, in_vmem],...  1.54 us

profile of v7, /device:TPU:257, one launch (start us, length us, event | category | flops | bytes accessed | tf_op | source)
XLA Modules:
  0.0 28.3 jit_solution(2907745572656999547)
XLA Ops:
  0.6 26.1 %contacts.1 = (f32[5,16,256]{2,1,0:T(8,128)}, f32[5,2,16]{2,1,0:T(2,128)}) custom-call(s32[1024,128]{1,0:T(8,128)} %bitcast.5, s32[1,256]{1,0:T(1,128)} %bitcast.7, bf16[96,8192]{1,0:T(8,128)(2,1)} %stem_hbm.1, bf16[6,48,288]{2,1,0:T(8,128)(2,1)} %trunk_in_hbm.1, bf16[6,48,96]{2,1,0:T(8,128)(2,1)} %bitcast.6, bf16[96,96]{1,0:T(8,128)(2,1)} %pair_hbm.1, ...), custom_call_target="tpu_custom_call" | custom-call | tf_op jit(solution)/shard_map/contacts/pallas_call | solution.py:473
  26.7 1.5 %hand_over.1 = (f32[5,16,256]{2,1,0:T(8,128)}, f32[5,2,16]{2,1,0:T(2,128)}) custom-call(f32[5,16,256]{2,1,0:T(8,128)} %get-tuple-element.6.band, f32[5,2,16]{2,1,0:T(2,128)} %get-tuple-element.7.scores), custom_call_target="tpu_custom_call" | custom-call | tf_op jit(solution)/shard_map/hand_over/pallas_call | solution.py:535
